TPU v7x, 128 devices: a whole 4x4x4 slice. The times are simulated.
128 devices in a mesh: leaf: 64 (over z, y_hi, x, core), cols: 2 (over y_lo).
Axes of the slice: x: 4, y: 4 (y_hi: 2, y_lo: 2; y = y_hi * 2 + y_lo), z: 4, core: 2. Of those that a mesh axis runs over, the one named last changes fastest.
Arguments:
- coordinates: float32 [64, 262144], P('cols', 'leaf'), may hold values from -6 to 6
- lengthscale: float32 [64], P('cols'), may hold values from 3 to 12
- tree_order: int32 [64, 4096], P('leaf'), may hold values from 0 to 4095, each once within a row
- probes: bfloat16 [262144, 512], P('leaf', 'cols'), may hold values from -6 to 6
- left_basis: bfloat16 [8, 96, 262144], P(None, None, 'leaf'), may hold values from -0.625 to 0.625
- right_basis: bfloat16 [8, 96, 262144], P(None, None, 'leaf'), may hold values from -6 to 6
Outputs:
- applied: float32 [262144, 512], P('leaf', 'cols')
Inputs may be any that keep to these rules, and one draw needn't show every extreme that they name: Each row of tree_order names each of the 4096 points of its block once.
All inputs are finite; a program needn't handle non-finite values.
Results may differ from a plain program's by a relative error of at most 0.0028.
Values sent between devices are 32-bit elements; how exact they have to be, the bound alone decides.
No kernel may reach another device: no remote copies, remote signals or barrier semaphores. Data moves between devices by JAX's collectives and lax.ppermute only.
A program may use at most 128 MiB of HBM per device.

v0:
```python
import math

import jax
import jax.numpy as jnp
from jax import lax
from jax.sharding import PartitionSpec as P

DIM = 64
RANK = 96
LEAF = 1024
LOCAL_LEVELS = 2


def laid_out(parts, dim):
    parts = jnp.moveaxis(parts, 0, dim)
    shape = parts.shape
    return parts.reshape(*shape[:dim], shape[dim] * shape[dim + 1], *shape[dim + 2 :])


def from_everyone(shard, axis):
    copies = jnp.broadcast_to(shard, (lax.axis_size(axis), *shard.shape))
    return lax.all_to_all(copies, axis, split_axis=0, concat_axis=0, tiled=True)


def gathered_copies(shard, axis, dim):
    return laid_out(from_everyone(shard, axis), dim)


def from_partner(value, axis, distance):
    mask = 2**distance
    pairs = [(source, source ^ mask) for source in range(lax.axis_size(axis))]
    return lax.ppermute(value, axis, pairs)


def local(coordinates, lengthscale, tree_order, probes, left_basis, right_basis):
    ordering = tree_order[0]
    points = probes.shape[0]
    columns = probes.shape[1]
    positions = jnp.arange(points, dtype=jnp.int32)
    inverse = jnp.zeros((points,), jnp.int32).at[ordering].set(positions)
    scaled = gathered_copies(coordinates / lengthscale[:, None], "cols", 0)
    scaled = jnp.take(scaled, ordering, axis=1)
    values = jnp.take(probes, ordering, axis=0)
    leaves = points // LEAF
    crossing = lax.axis_size("leaf").bit_length() - 1
    grouped = scaled.reshape(DIM, leaves, LEAF)
    gram_tile = jnp.einsum(
        "dnp,dnq->npq",
        grouped,
        grouped,
        precision=lax.Precision.HIGHEST,
        preferred_element_type=jnp.float32,
    )
    squared = jnp.sum(grouped * grouped, axis=0)
    kernel = jnp.exp(-0.5 * (squared[:, :, None] + squared[:, None, :] - 2.0 * gram_tile)).astype(
        jnp.bfloat16
    )
    result = jnp.einsum(
        "npq,nqc->npc",
        kernel,
        values.reshape(leaves, LEAF, columns),
        preferred_element_type=jnp.float32,
    ).reshape(points, columns)
    partials = jnp.einsum(
        "lrp,pc->lrc", right_basis[:crossing], values, preferred_element_type=jnp.float32
    )
    received = [partials[0]] * crossing
    pending = partials
    for which_bit in range(crossing):
        active = crossing - which_bit
        incoming = from_partner(pending, "leaf", which_bit)
        received[active - 1] = incoming[active - 1]
        pending = pending[: active - 1] + incoming[: active - 1]
    scales = jnp.array(
        [1.0 / math.sqrt(points * 2 ** (crossing - height)) for height in range(1, crossing + 1)],
        jnp.float32,
    )
    coefficient = (jnp.stack(received) * scales[:, None, None]).astype(jnp.bfloat16)
    result = result + jnp.einsum(
        "lrp,lrc->pc", left_basis[:crossing], coefficient, preferred_element_type=jnp.float32
    )
    for inside in range(1, LOCAL_LEVELS + 1):
        node_count = 2**inside
        node_size = points // node_count
        right_part = right_basis[crossing + inside - 1].reshape(RANK, node_count, node_size)
        local_coef = jnp.einsum(
            "rnm,nmc->nrc",
            right_part,
            values.reshape(node_count, node_size, columns),
            preferred_element_type=jnp.float32,
        )
        local_coef = (local_coef * (1.0 / math.sqrt(node_size))).astype(jnp.bfloat16)
        sibling = jnp.flip(local_coef.reshape(node_count // 2, 2, RANK, columns), axis=1).reshape(
            node_count, RANK, columns
        )
        left_part = left_basis[crossing + inside - 1].reshape(RANK, node_count, node_size)
        result = result + jnp.einsum(
            "rnm,nrc->nmc", left_part, sibling, preferred_element_type=jnp.float32
        ).reshape(points, columns)
    return jnp.take(result, inverse, axis=0)


def solution(mesh):
    placed = (
        P("cols", "leaf"),
        P("cols"),
        P("leaf", None),
        P("leaf", "cols"),
        P(None, None, "leaf"),
        P(None, None, "leaf"),
    )
    return jax.shard_map(
        local, mesh=mesh, in_specs=placed, out_specs=P("leaf", "cols"), check_vma=False
    )
```

profile of v0, /device:TPU:0, one launch (start us, length us, event | category | flops | bytes accessed | tf_op | source)
XLA Modules:
  0.0 184.4 jit_solution(12522048577128088796)
XLA Ops:
  0.0 0.0 copy-start
  0.0 0.9 compare_select_fusion
  0.9 0.7 compare_and_fusion.2
  1.6 0.0 copy-done
  1.6 0.0 copy-start.8
  1.6 16.9 %gather_fusion.1 = bf16[4096,256]{1,0:T(8,128)(2,1)} fusion(bf16[4096,256]{1,0:T(8,128)(2,1)S(1)} %copy-done, s32[4096]{0:T(1024)S(1)} %broadcast_clamp_fusion), kind=kCustom, calls=%fused_computation.1 | custom fusion | bytes 4210688 | tf_op jit(solution)/shard_map/jit(_take)/gather | solution.py:43
  18.6 0.0 copy-done.8
  18.6 5.4 %fusion.17 = f32[6,96,256]{2,1,0:T(8,128)} fusion(bf16[8,96,4096]{2,1,0:T(8,128)(2,1)} %param.12, bf16[4096,256]{1,0:T(8,128)(2,1)} %gather_fusion.1, pred[4096]{0:T(1024)(128)(4,1)S(1)} %compare_and_fusion.2), kind=kOutput, calls=%fused_computation.28 | convolution fusion | flops 1209008128 | bytes 7409664 | tf_op jit(solution)/shard_map/lrp,pc->lrc/dot_general | solution.py:64
  24.0 0.0 collective-permute-start
  24.0 0.0 copy-done.5
  24.0 0.0 copy-done.14
  24.0 0.1 broadcast_divide_fusion
  24.1 1.1 broadcast_in_dim.54
  25.2 3.6 %all-to-all-start = ((f32[2,32,4096]{2,1,0:T(8,128)}), f32[2,32,4096]{2,1,0:T(8,128)S(1)}, u32[]{:S(2)}, u32[]{:S(2)}) async-start(f32[2,32,4096]{2,1,0:T(8,128)} %broadcast_in_dim.54), calls=%async_computation | async-start | bytes 2097152 | tf_op jit(solution)/shard_map/all_to_all | solution.py:22
  28.7 1.5 fusion.53
  30.3 0.0 copy-done.7
  30.3 0.5 broadcast.94
  30.8 0.7 reduce.6
  31.5 1.5 reshape_squeeze.14
  33.0 2.4 %fusion.52 = (bf16[1,96,4096]{2,1,0:T(8,128)(2,1)}, bf16[1,96,4096]{2,1,0:T(8,128)(2,1)S(1)}) fusion(bf16[8,96,4096]{2,1,0:T(8,128)(2,1)} %param.11), kind=kLoop, calls=%fused_computation.76 | loop fusion | bytes 3145728 | tf_op jit(solution)/shard_map/slice | solution.py:96
  35.4 1.5 reshape_squeeze.12
  36.9 15.5 %scatter_custom_fusion = s32[4096]{0:T(1024)S(1)} fusion(s32[4096]{0:T(1024)S(1)} %bitcast.64, s32[4096]{0:T(1024)S(1)} %iota.3, s32[]{:T(128)} %constant.25.clone.1), kind=kCustom, calls=%fused_computation.69 | custom fusion | bytes 16388 | tf_op jit(solution)/shard_map/scatter | solution.py:40
  52.4 0.0 copy-start.2
  52.5 0.0 collective-permute-done
  52.5 1.4 slice_add_fusion
  53.9 1.7 collective-permute-start.1
  55.6 2.7 %fusion.23 = bf16[4,256,96]{1,2,0:T(8,128)(2,1)S(1)} fusion(bf16[4,1024,256]{2,1,0:T(8,128)(2,1)} %bitcast.56, pred[4,1024]{1,0:T(4,128)(4,1)S(1)} %compare_and_fusion.1, bf16[96,4,1024]{2,1,0:T(4,128)(2,1)} %reshape_squeeze.14), kind=kOutput, calls=%fused_computation.30 | convolution fusion | flops 202571776 | bytes 3084288 | tf_op jit(solution)/shard_map/rnm,nmc->nrc/dot_general | solution.py:86
  58.3 1.9 %fusion.30 = bf16[2,96,256]{2,1,0:T(8,128)(2,1)} fusion(bf16[2,2048,256]{2,1,0:T(8,128)(2,1)S(1)} %bitcast.57, pred[2,2048]{1,0:T(4,128)(4,1)S(1)} %compare_and_fusion, bf16[96,2,2048]{2,1,0:T(2,128)(2,1)S(1)} %copy-done.4), kind=kOutput, calls=%fused_computation.33 | convolution fusion | flops 202473472 | bytes 2985984 | tf_op jit(solution)/shard_map/rnm,nmc->nrc/dot_general | solution.py:86
  60.1 7.4 %collective-permute-done.1 = f32[5,96,256]{2,1,0:T(8,128)S(1)} collective-permute-done((f32[5,96,256]{2,1,0:T(8,128)S(1)}, f32[5,96,256]{2,1,0:T(8,128)S(1)}, u32[]{:S(2)}, u32[]{:S(2)}) %collective-permute-start.1) | collective-permute-done | bytes 491552 | tf_op jit(solution)/shard_map/ppermute | solution.py:32
  67.6 0.1 slice_add_fusion.1
  67.6 3.2 %collective-permute-start.2 = (f32[4,96,256]{2,1,0:T(8,128)S(1)}, f32[4,96,256]{2,1,0:T(8,128)}, u32[]{:S(2)}, u32[]{:S(2)}) collective-permute-start(f32[4,96,256]{2,1,0:T(8,128)S(1)} %slice_add_fusion.1), channel_id=1, source_target_pairs={{0,8},{2,10},{4,12},{6,14},{8,0},{10,2},{12,4},{14,6},{16,24},{18,... | collective-permute-start | bytes 1179656 | tf_op jit(solution)/shard_map/ppermute | solution.py:32
  70.9 0.6 compare_and_fusion.3
  71.5 0.0 copy-done.6
  71.5 0.6 reshape_squeeze.15
  72.0 0.9 reshape.93
  72.9 2.6 %reshape_squeeze.13 = bf16[96,2,2048]{2,1,0:T(2,128)(2,1)S(1)} reshape(bf16[1,96,4096]{2,1,0:T(8,128)(2,1)} %get-tuple-element.5) | data formatting | bytes 1572864 | tf_op jit(solution)/shard_map/reshape;squeeze | solution.py:96
  75.5 0.8 convolution_bitcast_fusion.2
  76.3 3.7 %collective-permute-done.2 = f32[4,96,256]{2,1,0:T(8,128)} collective-permute-done((f32[4,96,256]{2,1,0:T(8,128)S(1)}, f32[4,96,256]{2,1,0:T(8,128)}, u32[]{:S(2)}, u32[]{:S(2)}) %collective-permute-start.2) | collective-permute-done | bytes 393248 | tf_op jit(solution)/shard_map/ppermute | solution.py:32
  80.0 1.0 slice_add_fusion.2
  81.0 3.6 %collective-permute-start.3 = (f32[3,96,256]{2,1,0:T(8,128)S(1)}, f32[3,96,256]{2,1,0:T(8,128)}, u32[]{:S(2)}, u32[]{:S(2)}) collective-permute-start(f32[3,96,256]{2,1,0:T(8,128)S(1)} %slice_add_fusion.2), channel_id=1, source_target_pairs={{0,16},{2,18},{4,20},{6,22},{8,24},{10,26},{12,28},{14,30},{16,0},... | collective-permute-start | bytes 884744 | tf_op jit(solution)/shard_map/ppermute | solution.py:32
  84.6 0.8 convolution_bitcast_fusion.1
  85.4 2.3 %copy.23 = f32[4,32,8,1024]{3,2,0,1:T(8,128)} copy(f32[4,32,8,1024]{3,2,1,0:T(8,128)S(1)} %convolution_bitcast_fusion.2) | data formatting | bytes 8388608 | tf_op jit(solution)/shard_map/reshape | solution.py:99
  87.7 2.2 %copy.22 = f32[2,32,8,2048]{3,2,0,1:T(8,128)} copy(f32[2,32,8,2048]{3,2,1,0:T(8,128)S(1)} %convolution_bitcast_fusion.1) | data formatting | bytes 8388608 | tf_op jit(solution)/shard_map/reshape | solution.py:99
  89.9 0.0 all-to-all-done
  89.9 0.6 copy.13
  90.5 14.1 %gather_fusion = f32[4096,64]{1,0:T(8,128)} fusion(f32[64,4096]{0,1:T(8,128)S(1)} %copy.13, s32[4096]{0:T(1024)S(1)} %broadcast_clamp_fusion), kind=kCustom, calls=%fused_computation | custom fusion | bytes 2113536 | tf_op jit(solution)/shard_map/jit(_take)/gather | solution.py:42
  104.7 2.5 %fusion.8 = f32[4096]{0:T(1024)S(1)} fusion(f32[4096,64]{1,0:T(8,128)} %gather_fusion, pred[4096]{0:T(1024)(128)(4,1)S(1)} %copy-done.9), kind=kLoop, calls=%fused_computation.17 | loop fusion | flops 782336 | bytes 1069056 | tf_op jit(solution)/shard_map/reduce_sum | solution.py:54
  107.2 0.0 collective-permute-done.3
  107.2 1.0 slice_add_fusion.3
  108.2 2.0 %collective-permute-start.4 = (f32[2,96,256]{2,1,0:T(8,128)S(1)}, f32[2,96,256]{2,1,0:T(8,128)S(1)}, u32[]{:S(2)}, u32[]{:S(2)}) collective-permute-start(f32[2,96,256]{2,1,0:T(8,128)S(1)} %slice_add_fusion.3), channel_id=1, source_target_pairs={{0,32},{2,34},{4,36},{6,38},{8,40},{10,42},{12,44},{14,46},{16,48}... | collective-permute-start | bytes 589832 | tf_op jit(solution)/shard_map/ppermute | solution.py:32
  110.2 18.7 %exponential_convert_fusion = bf16[4,1024,1024]{2,1,0:T(8,128)(2,1)S(1)} fusion(f32[4,1024]{1,0:T(4,128)S(1)} %reduce_sum.12, f32[64,4,1024]{0,2,1:T(8,128)} %bitcast.53, pred[4,1024]{1,0:T(4,128)(4,1)S(1)} %copy-done.12), kind=kOutput, calls=%fused_computation.4 | convolution fusion | flops 3242459136 | bytes 9457664 | tf_op jit(solution)/shard_map/dnp,dnq->npq/dot_general | solution.py:47
  128.9 0.0 collective-permute-done.4
  128.9 3.9 %collective-permute-start.5 = (f32[1,96,256]{2,1,0:T(8,128)S(1)}, f32[1,96,256]{2,1,0:T(8,128)S(1)}, u32[]{:S(2)}, u32[]{:S(2)}) collective-permute-start(f32[1,96,256]{2,1,0:T(8,128)S(1)} %slice_add_fusion.4), channel_id=1, source_target_pairs={{0,64},{2,66},{4,68},{6,70},{8,72},{10,74},{12,76},{14,78},{16,80}... | collective-permute-start | bytes 294920 | tf_op jit(solution)/shard_map/ppermute | solution.py:32
  132.8 4.1 %fusion.16 = f32[4,1024,256]{2,1,0:T(8,128)} fusion(bf16[4,1024,1024]{2,1,0:T(8,128)(2,1)S(1)} %exponential_convert_fusion, bf16[4,1024,256]{2,1,0:T(8,128)(2,1)S(1)} %bitcast.58, pred[4,1024]{1,0:T(4,128)(4,1)S(1)} %copy-done.12), kind=kOutput, calls=%fused_computation.27 | convolution fusion | flops 2148532224 | bytes 14684160 | tf_op jit(solution)/shard_map/npq,nqc->npc/dot_general | solution.py:58
  136.9 5.7 %copy.14 = f32[4096,256]{0,1:T(8,128)} copy(f32[4096,256]{1,0:T(8,128)} %bitcast.55) | data formatting | bytes 8388608 | tf_op jit(solution)/shard_map/reshape | solution.py:63
  142.6 0.0 collective-permute-done.5
  142.6 0.9 slice_dynamic-update-slice_fusion.3
  143.5 0.9 slice_dynamic-update-slice_fusion.2
  144.4 0.9 slice_dynamic-update-slice_fusion.1
  145.3 0.9 slice_dynamic-update-slice_fusion
  146.2 10.2 %fusion.2 = f32[4096,256]{0,1:T(8,128)} fusion(f32[4096,256]{0,1:T(8,128)} %bitcast.51, f32[4096,256]{0,1:T(8,128)} %bitcast.52, f32[4096,256]{0,1:T(8,128)} %copy.14, bf16[8,96,4096]{2,1,0:T(8,128)(2,1)} %param.11, f32[6,96,256]{2,1,0:T(8,128)S(1)} %slice_dynamic-update-slice_fusion, f32[6]{0:T(128)S(1)} %copy-done.13), kind=kOutput, calls=%fused_computation.8 | convolution fusion | flops 1211400192 | bytes 22085656 | tf_op jit(solution)/shard_map/lrp,lrc->pc/dot_general | solution.py:79
  156.4 5.6 %copy.20 = f32[4096,256]{1,0:T(8,128)} copy(f32[4096,256]{0,1:T(8,128)} %fusion.2) | data formatting | bytes 8388608 | tf_op jit(solution)/shard_map/add | solution.py:97
  162.0 18.5 %gather_fusion.2 = f32[4096,256]{1,0:T(8,128)} fusion(f32[4096,256]{1,0:T(8,128)} %copy.20, s32[4096]{0:T(1024)S(1)} %fusion.44), kind=kCustom, calls=%fused_computation.2 | custom fusion | bytes 8404992 | tf_op jit(solution)/shard_map/jit(_take)/gather | solution.py:100
  180.5 3.9 %broadcast_select_fusion = f32[4096,256]{1,0:T(8,128)} fusion(f32[4096,256]{1,0:T(8,128)} %gather_fusion.2, pred[4096]{0:T(1024)(128)(4,1)S(1)} %copy-done.10), kind=kLoop, calls=%fused_computation.18 | loop fusion | flops 1048576 | bytes 8392704 | tf_op jit(solution)/shard_map/jit(_take)/select_n | solution.py:100
  (33 shorter events, 0.2 us)
Async XLA Ops:
  0.0 1.6 copy-start
  1.6 16.9 %copy-start.8 = (pred[4096]{0:T(1024)(128)(4,1)}, pred[4096]{0:T(1024)(128)(4,1)S(1)}, u32[]{:S(2)}) copy-start(pred[4096]{0:T(1024)(128)(4,1)S(1)} %compare_and_fusion.2) | copy-start | bytes 12292
  18.6 5.4 %copy-start.5 = (f32[32,4096]{1,0:T(8,128)S(1)}, f32[32,4096]{1,0:T(8,128)}, u32[]{:S(2)}) copy-start(f32[32,4096]{1,0:T(8,128)} %param.7) | copy-start | bytes 1572868
  18.6 5.4 %copy-start.14 = (f32[32]{0:T(128)S(1)}, f32[32]{0:T(128)}, u32[]{:S(2)}) copy-start(f32[32]{0:T(128)} %param.8) | copy-start | bytes 388
  24.0 6.3 %copy-start.7 = (s32[1,4096]{1,0:T(1,128)S(1)}, s32[1,4096]{1,0:T(1,128)}, u32[]{:S(2)}) copy-start(s32[1,4096]{1,0:T(1,128)} %param.9) | copy-start | bytes 49156
  24.0 28.5 %collective-permute-start = (f32[6,96,256]{2,1,0:T(8,128)}, f32[6,96,256]{2,1,0:T(8,128)}, u32[]{:S(2)}, u32[]{:S(2)}) collective-permute-start(f32[6,96,256]{2,1,0:T(8,128)} %fusion.17), channel_id=1, source_target_pairs={{0,2},{2,0},{4,6},{6,4},{8,10},{10,8},{12,14},{14,12},{16,18},{18,... | collective-permute-start | bytes 1769480 | tf_op jit(solution)/shard_map/ppermute | solution.py:32
  25.2 64.8 %all-to-all-start = ((f32[2,32,4096]{2,1,0:T(8,128)}), f32[2,32,4096]{2,1,0:T(8,128)S(1)}, u32[]{:S(2)}, u32[]{:S(2)}) async-start(f32[2,32,4096]{2,1,0:T(8,128)} %broadcast_in_dim.54), calls=%async_computation | async-start | bytes 2097152 | tf_op jit(solution)/shard_map/all_to_all | solution.py:22
  36.9 21.4 %copy-start.4 = (bf16[96,2,2048]{2,1,0:T(2,128)(2,1)S(1)}, bf16[96,2,2048]{2,1,0:T(2,128)(2,1)}, u32[]{:S(2)}) copy-start(bf16[96,2,2048]{2,1,0:T(2,128)(2,1)} %reshape_squeeze.12) | copy-start | bytes 2359300
  52.4 5.9 %copy-start.2 = (bf16[4096,256]{1,0:T(8,128)(2,1)S(1)}, bf16[4096,256]{1,0:T(8,128)(2,1)}, u32[]{:S(2)}) copy-start(bf16[4096,256]{1,0:T(8,128)(2,1)} %gather_fusion.1) | copy-start | bytes 6291460
  52.4 7.7 %copy-start.11 = (pred[4,1024]{1,0:T(4,128)(4,1)}, pred[4,1024]{1,0:T(4,128)(4,1)S(1)}, u32[]{:S(2)}) copy-start(pred[4,1024]{1,0:T(4,128)(4,1)S(1)} %compare_and_fusion.1) | copy-start | bytes 12292
  53.9 13.7 %collective-permute-start.1 = (f32[5,96,256]{2,1,0:T(8,128)S(1)}, f32[5,96,256]{2,1,0:T(8,128)S(1)}, u32[]{:S(2)}, u32[]{:S(2)}) collective-permute-start(f32[5,96,256]{2,1,0:T(8,128)S(1)} %slice_add_fusion), channel_id=1, source_target_pairs={{0,4},{2,6},{4,0},{6,2},{8,12},{10,14},{12,8},{14,10},{16,20},{18,... | collective-permute-start | bytes 1474568 | tf_op jit(solution)/shard_map/ppermute | solution.py:32
  67.6 3.9 %copy-start.6 = (f32[5,96,256]{2,1,0:T(8,128)}, f32[5,96,256]{2,1,0:T(8,128)S(1)}, u32[]{:S(2)}) copy-start(f32[5,96,256]{2,1,0:T(8,128)S(1)} %collective-permute-done.1) | copy-start | bytes 1474564
  67.6 12.3 %collective-permute-start.2 = (f32[4,96,256]{2,1,0:T(8,128)S(1)}, f32[4,96,256]{2,1,0:T(8,128)}, u32[]{:S(2)}, u32[]{:S(2)}) collective-permute-start(f32[4,96,256]{2,1,0:T(8,128)S(1)} %slice_add_fusion.1), channel_id=1, source_target_pairs={{0,8},{2,10},{4,12},{6,14},{8,0},{10,2},{12,4},{14,6},{16,24},{18,... | collective-permute-start | bytes 1179656 | tf_op jit(solution)/shard_map/ppermute | solution.py:32
  81.0 26.2 %collective-permute-start.3 = (f32[3,96,256]{2,1,0:T(8,128)S(1)}, f32[3,96,256]{2,1,0:T(8,128)}, u32[]{:S(2)}, u32[]{:S(2)}) collective-permute-start(f32[3,96,256]{2,1,0:T(8,128)S(1)} %slice_add_fusion.2), channel_id=1, source_target_pairs={{0,16},{2,18},{4,20},{6,22},{8,24},{10,26},{12,28},{14,30},{16,0},... | collective-permute-start | bytes 884744 | tf_op jit(solution)/shard_map/ppermute | solution.py:32
  90.5 14.2 %copy-start.9 = (pred[4096]{0:T(1024)(128)(4,1)S(1)}, pred[4096]{0:T(1024)(128)(4,1)}, u32[]{:S(2)}) copy-start(pred[4096]{0:T(1024)(128)(4,1)} %copy-done.8) | copy-start | bytes 12292
  90.5 19.6 %copy-start.12 = (pred[4,1024]{1,0:T(4,128)(4,1)S(1)}, pred[4,1024]{1,0:T(4,128)(4,1)}, u32[]{:S(2)}) copy-start(pred[4,1024]{1,0:T(4,128)(4,1)} %copy-done.11) | copy-start | bytes 12292
  108.2 20.7 %collective-permute-start.4 = (f32[2,96,256]{2,1,0:T(8,128)S(1)}, f32[2,96,256]{2,1,0:T(8,128)S(1)}, u32[]{:S(2)}, u32[]{:S(2)}) collective-permute-start(f32[2,96,256]{2,1,0:T(8,128)S(1)} %slice_add_fusion.3), channel_id=1, source_target_pairs={{0,32},{2,34},{4,36},{6,38},{8,40},{10,42},{12,44},{14,46},{16,48}... | collective-permute-start | bytes 589832 | tf_op jit(solution)/shard_map/ppermute | solution.py:32
  110.2 22.7 %copy-start.3 = (bf16[4096,256]{1,0:T(8,128)(2,1)S(1)}, bf16[4096,256]{1,0:T(8,128)(2,1)}, u32[]{:S(2)}) copy-start(bf16[4096,256]{1,0:T(8,128)(2,1)} %gather_fusion.1) | copy-start | bytes 6291460
  128.9 13.6 %collective-permute-start.5 = (f32[1,96,256]{2,1,0:T(8,128)S(1)}, f32[1,96,256]{2,1,0:T(8,128)S(1)}, u32[]{:S(2)}, u32[]{:S(2)}) collective-permute-start(f32[1,96,256]{2,1,0:T(8,128)S(1)} %slice_add_fusion.4), channel_id=1, source_target_pairs={{0,64},{2,66},{4,68},{6,70},{8,72},{10,74},{12,76},{14,78},{16,80}... | collective-permute-start | bytes 294920 | tf_op jit(solution)/shard_map/ppermute | solution.py:32
  136.9 9.3 %copy-start.13 = (f32[6]{0:T(128)S(1)}, f32[6]{0:T(128)}, u32[]{:S(2)}) copy-start(f32[6]{0:T(128)} %constant.55.clone) | copy-start | bytes 76
  162.0 18.5 %copy-start.10 = (pred[4096]{0:T(1024)(128)(4,1)S(1)}, pred[4096]{0:T(1024)(128)(4,1)}, u32[]{:S(2)}) copy-start(pred[4096]{0:T(1024)(128)(4,1)} %compare_and_fusion.3) | copy-start | bytes 12292
  162.0 22.4 %copy-start.1 = (bf16[4096,256]{1,0:T(8,128)(2,1)S(1)}, bf16[4096,256]{1,0:T(8,128)(2,1)}, u32[]{:S(2)}) copy-start(bf16[4096,256]{1,0:T(8,128)(2,1)} %param.10) | copy-start | bytes 6291460
where the time goes:
time: 185 us; the launch traced here: 184 us
  local copies, waits for them, and re-layouts  97.7 us (53%)
  matrix products  44.5 us (24%)
  starting transfers between devices  17.9 us (10%)
  other arithmetic  12.9 us (7%)
  waiting for transfers between devices  11.1 us (6%)
    dot_general x1, matrix products, local(): jnp.einsum('dnp,dnq->npq', grouped, grouped, precision=lax.Precision.HIGH...  18.7 us
    gather x1, local copies, waits for them, and re-layouts, local(): return jnp.take(result, inverse, axis=0)  18.5 us
    gather x1, local copies, waits for them, and re-layouts, local(): values = jnp.take(probes, ordering, axis=0)  16.9 us
    scatter x1, local copies, waits for them, and re-layouts, local(): inverse = jnp.zeros((points,), jnp.int32).at[ordering].set(positions)  15.5 us
    ppermute x6, starting transfers between devices, from_partner(): return lax.ppermute(value, axis, pairs)  14.4 us
    gather x1, local copies, waits for them, and re-layouts, local(): scaled = jnp.take(scaled, ordering, axis=1)  14.1 us
    ppermute x6, waiting for transfers between devices, from_partner(): return lax.ppermute(value, axis, pairs)  11.1 us
    dot_general x1, matrix products, local(): jnp.einsum('lrp,lrc->pc', left_basis[:crossing], coefficient, preferred_e...  10.2 us
  transfers between devices with their start and end apart: 7, of which 2 were waited for; matrix products, arithmetic and copies ran while one was open for 48% of the time, Pallas kernels for 0%

commit v1 on v0

v1 whole, which is shorter than its diff:
```python
import functools
import math

import jax
import jax.numpy as jnp
from jax import lax
from jax.experimental import pallas as pl
from jax.experimental.pallas import tpu as pltpu
from jax.sharding import PartitionSpec as P

DIM = 64
RANK = 96
LEAF = 1024
CROSS = 6
PTS = 4096
COLS = 256
LEAVES = PTS // LEAF
ROOT = math.sqrt(math.log2(math.e))
F32 = jnp.float32
BF16 = jnp.bfloat16
VM = 64 * 1024 * 1024 - 2 * 1024 * 1024


def whole(shape):
    return pl.BlockSpec(shape, lambda *_: (0,) * len(shape))


def move_rows(order, source, target, width, scatter, unroll=16):
    def group(step, carry):
        for k in range(unroll):
            t = step * unroll + k
            far = order[t]
            near = t
            take, put = (near, far) if scatter else (far, near)
            target[pl.ds(put * width, width), :] = source[pl.ds(take * width, width), :]
        return carry

    lax.fori_loop(0, PTS // unroll, group, 0)


def right_kernel(order, core, probes, right, values, send, keep, coef7, coef8, rows, moved, acc):
    def spread(step, carry):
        base = step * 16
        block = probes[pl.ds(base, 16), :].astype(F32)
        rows[pl.ds(2 * base, 16, stride=2), :] = block[:, :128]
        rows[pl.ds(2 * base + 1, 16, stride=2), :] = block[:, 128:]
        return carry

    lax.fori_loop(0, PTS // 16, spread, 0, unroll=4)
    move_rows(order, rows, moved, 2, False)

    def gather_back(step, carry):
        base = step * 16
        low = moved[pl.ds(2 * base, 16, stride=2), :]
        high = moved[pl.ds(2 * base + 1, 16, stride=2), :]
        values[pl.ds(base, 16), :] = jnp.concatenate([low, high], axis=1).astype(BF16)
        return carry

    lax.fori_loop(0, PTS // 16, gather_back, 0, unroll=4)
    half = []
    for leaf in range(LEAVES):
        span = pl.ds(leaf * LEAF, LEAF)
        part = jnp.dot(
            right[:, :, span].reshape(8 * RANK, LEAF), values[span, :], preferred_element_type=F32
        )
        if leaf == 0:
            acc[...] = part[: CROSS * RANK]
        else:
            acc[...] += part[: CROSS * RANK]
        coef8[leaf] = (part[7 * RANK :] * (1.0 / math.sqrt(LEAF))).astype(BF16)
        half.append(part[6 * RANK : 7 * RANK])
    for node in range(2):
        total = half[2 * node] + half[2 * node + 1]
        coef7[node] = (total * (1.0 / math.sqrt(2 * LEAF))).astype(BF16)

    def level(bit):
        return acc[pl.ds((CROSS - 1 - bit) * RANK, RANK), :]

    send[0] = level(0)

    @pl.when(core[0] == 0)
    def _():
        for k in range(3):
            send[1 + k] = level(1 + k)
        keep[0] = level(4)
        keep[1] = level(5)
        keep[2] = jnp.zeros((RANK, COLS), F32)

    @pl.when(core[0] == 1)
    def _():
        for k in range(3):
            keep[k] = level(1 + k)
        send[1] = level(4)
        send[2] = level(5)
        send[3] = jnp.zeros((RANK, COLS), F32)


def right_stage(order, core, probes, right):
    smem = pl.BlockSpec(memory_space=pltpu.SMEM)
    return pl.pallas_call(
        right_kernel,
        out_shape=(
            jax.ShapeDtypeStruct((PTS, COLS), BF16),
            jax.ShapeDtypeStruct((4, RANK, COLS), F32),
            jax.ShapeDtypeStruct((3, RANK, COLS), F32),
            jax.ShapeDtypeStruct((2, RANK, COLS), BF16),
            jax.ShapeDtypeStruct((4, RANK, COLS), BF16),
        ),
        in_specs=[smem, smem, whole((PTS, COLS)), whole((8, RANK, PTS))],
        out_specs=(
            whole((PTS, COLS)),
            whole((4, RANK, COLS)),
            whole((3, RANK, COLS)),
            whole((2, RANK, COLS)),
            whole((4, RANK, COLS)),
        ),
        scratch_shapes=[
            pltpu.VMEM((2 * PTS, 128), F32),
            pltpu.VMEM((2 * PTS, 128), F32),
            pltpu.VMEM((CROSS * RANK, COLS), F32),
        ],
        compiler_params=pltpu.CompilerParams(vmem_limit_bytes=VM),
        cost_estimate=pl.CostEstimate(
            flops=2 * 768 * PTS * COLS, bytes_accessed=12 << 20, transcendentals=0
        ),
        name="right_stage",
    )(order, core, probes, right)


def points_kernel(order, own, other, left, right, rows, moved):
    def turn(step, carry):
        span = pl.ds(pl.multiple_of(step * 128, 128), 128)
        tile = jnp.concatenate([own[:, span], other[:, span]], axis=0) * ROOT
        rows[span, :] = jnp.concatenate([tile, tile], axis=0).T
        return carry

    lax.fori_loop(0, PTS // 128, turn, 0, unroll=2)
    move_rows(order, rows, moved, 1, False)

    def split(step, carry):
        span = pl.ds(pl.multiple_of(step * 32, 32), 32)
        x = moved[span, :]
        lane = lax.broadcasted_iota(jnp.int32, x.shape, 1)
        high = x.astype(BF16).astype(F32)
        low = x - high
        norm = jnp.sum(x * x, axis=1, keepdims=True) * -0.25
        first = norm.astype(BF16).astype(F32)
        second = (norm - first).astype(BF16).astype(F32)
        third = norm - first - second
        terms = jnp.where(lane % 3 == 0, second, jnp.where(lane % 3 == 1, first, third))
        one = jnp.ones_like(x)
        zero = jnp.zeros_like(x)
        early = lane < 67
        tail = lane < 70
        extra_left = jnp.where(early, terms, jnp.where(tail, one, zero))
        extra_right = jnp.where(early, one, jnp.where(tail, terms, zero))
        front = lane < DIM
        left[span, :] = jnp.concatenate([high, jnp.where(front, low, extra_left)], axis=1).astype(BF16)
        right[span, :] = jnp.concatenate(
            [jnp.where(front, high, low), jnp.where(front, high, extra_right)], axis=1
        ).astype(BF16)
        return carry

    lax.fori_loop(0, PTS // 32, split, 0, unroll=2)


def points_stage(order, own, other):
    return pl.pallas_call(
        points_kernel,
        out_shape=(
            jax.ShapeDtypeStruct((PTS, 256), BF16),
            jax.ShapeDtypeStruct((PTS, 256), BF16),
        ),
        in_specs=[
            pl.BlockSpec(memory_space=pltpu.SMEM),
            whole((DIM // 2, PTS)),
            whole((DIM // 2, PTS)),
        ],
        out_specs=(whole((PTS, 256)), whole((PTS, 256))),
        scratch_shapes=[pltpu.VMEM((PTS, 128), F32), pltpu.VMEM((PTS, 128), F32)],
        compiler_params=pltpu.CompilerParams(vmem_limit_bytes=VM),
        cost_estimate=pl.CostEstimate(flops=PTS * 4096, bytes_accessed=5 << 20, transcendentals=0),
        name="points_stage",
    )(order, own, other)


def near_kernel(left, right, values, basis, coef7, coef8, near):
    leaf = pl.program_id(0)
    block = 256
    coef = jnp.concatenate([coef7[...], coef8[...]], axis=0)
    for step in range(LEAF // block):
        span = pl.ds(step * block, block)
        power = lax.dot_general(
            left[span, :], right[...], (((1,), (1,)), ((), ())), preferred_element_type=F32
        )
        kernel = jnp.exp2(power).astype(BF16)
        total = jnp.dot(kernel, values[...], preferred_element_type=F32)
        total += lax.dot_general(
            basis[:, :, span].reshape(2 * RANK, block),
            coef,
            (((0,), (0,)), ((), ())),
            preferred_element_type=F32,
        )
        near[span, :] = total


def near_stage(left, right, values, basis, coef7, coef8):
    return pl.pallas_call(
        near_kernel,
        grid=(LEAVES,),
        out_shape=jax.ShapeDtypeStruct((PTS, COLS), F32),
        in_specs=[
            pl.BlockSpec((LEAF, 256), lambda i: (i, 0)),
            pl.BlockSpec((LEAF, 256), lambda i: (i, 0)),
            pl.BlockSpec((LEAF, COLS), lambda i: (i, 0)),
            pl.BlockSpec((2, RANK, LEAF), lambda i: (3, 0, i)),
            pl.BlockSpec((None, RANK, COLS), lambda i: (1 - i // 2, 0, 0)),
            pl.BlockSpec((None, RANK, COLS), lambda i: (i + 1 - 2 * (i % 2), 0, 0)),
        ],
        out_specs=pl.BlockSpec((LEAF, COLS), lambda i: (i, 0)),
        compiler_params=pltpu.CompilerParams(vmem_limit_bytes=VM),
        cost_estimate=pl.CostEstimate(
            flops=2 * PTS * LEAF * 512, bytes_accessed=12 << 20, transcendentals=PTS * LEAF
        ),
        name="near_stage",
    )(left, right, values, basis, coef7, coef8)


def finish_kernel(order, core, near, basis, zero, mine, theirs, fourth, fifth, out, coef, rows, moved):
    block = 256
    root = [1.0 / math.sqrt(PTS * 2**bit) for bit in range(CROSS)]

    def put(bit, value):
        coef[pl.ds((CROSS - 1 - bit) * RANK, RANK), :] = (value * root[bit]).astype(BF16)

    put(0, zero[...])

    @pl.when(core[0] == 0)
    def _():
        for k in range(3):
            put(1 + k, theirs[k])
        put(4, mine[0])
        put(5, mine[1])

    @pl.when(core[0] == 1)
    def _():
        for k in range(3):
            put(1 + k, mine[k])
        put(4, fourth[...])
        put(5, fifth[...])

    for step in range(PTS // block):
        span = pl.ds(step * block, block)
        total = near[span, :] + lax.dot_general(
            basis[:, :, span].reshape(CROSS * RANK, block),
            coef[...],
            (((0,), (0,)), ((), ())),
            preferred_element_type=F32,
        )
        rows[pl.ds(2 * step * block, block, stride=2), :] = total[:, :128]
        rows[pl.ds(2 * step * block + 1, block, stride=2), :] = total[:, 128:]
    move_rows(order, rows, moved, 2, True)

    def collect(step, carry):
        base = step * 8
        out[pl.ds(base, 8), :] = jnp.concatenate(
            [moved[pl.ds(2 * base, 8, stride=2), :], moved[pl.ds(2 * base + 1, 8, stride=2), :]], axis=1
        )
        return carry

    lax.fori_loop(0, PTS // 8, collect, 0, unroll=8)


def finish_stage(order, core, near, basis, zero, mine, theirs, fourth, fifth):
    smem = pl.BlockSpec(memory_space=pltpu.SMEM)
    return pl.pallas_call(
        finish_kernel,
        grid=(1,),
        out_shape=jax.ShapeDtypeStruct((PTS, COLS), F32),
        in_specs=[
            smem,
            smem,
            whole((PTS, COLS)),
            whole((CROSS, RANK, PTS)),
            whole((RANK, COLS)),
            whole((3, RANK, COLS)),
            whole((3, RANK, COLS)),
            whole((RANK, COLS)),
            whole((RANK, COLS)),
        ],
        out_specs=whole((PTS, COLS)),
        scratch_shapes=[
            pltpu.VMEM((CROSS * RANK, COLS), BF16),
            pltpu.VMEM((2 * PTS, 128), F32),
            pltpu.VMEM((2 * PTS, 128), F32),
        ],
        compiler_params=pltpu.CompilerParams(vmem_limit_bytes=VM),
        cost_estimate=pl.CostEstimate(
            flops=2 * 576 * PTS * COLS, bytes_accessed=16 << 20, transcendentals=0
        ),
        name="finish_stage",
    )(order, core, near, basis, zero, mine, theirs, fourth, fifth)


def swap(value, masks):
    pairs = []
    for source in range(64):
        mask = masks[source % 2]
        if mask:
            pairs.append((source, source ^ mask))
    return lax.ppermute(value, "leaf", pairs)


CORE, XA, XB, YB, ZA, ZB = 1, 2, 6, 8, 16, 48


def local(coordinates, lengthscale, tree_order, probes, left_basis, right_basis):
    order = tree_order[0]
    side = lax.axis_index("leaf") % 2
    core = side.reshape(1)
    scaled = coordinates / lengthscale[:, None]
    other = lax.ppermute(scaled, "cols", [(0, 1), (1, 0)])
    values, send, keep, coef7, coef8 = right_stage(order, core, probes, right_basis)
    got = swap(send, (CORE, CORE))
    zero = got[0]
    total = keep + got[1:]
    pair = swap(total[:2], (YB, XA))
    lone = swap(total[2], (0, XA))
    first = pair[0]
    pair = total[:2] + pair
    pair = jnp.where(side == 0, pair, jnp.stack([pair[1], total[2] + lone]))
    got = swap(pair, (XA, XB))
    second = got[0]
    pair = pair + got
    got = swap(pair, (XB, YB))
    third = got[1]
    pair = pair + got
    got = swap(pair, (ZA, 0))
    fourth = got[0]
    top = pair[1] + got[1]
    fifth = swap(top, (ZB, 0))
    low = jnp.stack([first, second, third])
    theirs = lax.ppermute(low, "leaf", [(s, s ^ 1) for s in range(64) if s % 2 == 1])
    fourth_in = lax.ppermute(fourth, "leaf", [(s, s ^ 1) for s in range(64) if s % 2 == 0])
    fifth_in = lax.ppermute(fifth, "leaf", [(s, s ^ 1) for s in range(64) if s % 2 == 0])
    mine = jnp.where(side == 0, jnp.stack([fourth, fifth, fifth]), low)
    point_left, point_right = points_stage(order, scaled, other)
    near = near_stage(point_left, point_right, values, left_basis, coef7, coef8)
    return finish_stage(order, core, near, left_basis, zero, mine, theirs, fourth_in, fifth_in)


def solution(mesh):
    placed = (
        P("cols", "leaf"),
        P("cols"),
        P("leaf", None),
        P("leaf", "cols"),
        P(None, None, "leaf"),
        P(None, None, "leaf"),
    )
    return jax.shard_map(
        local, mesh=mesh, in_specs=placed, out_specs=P("leaf", "cols"), check_vma=False
    )
```

time: 185 us -> 99.6 us (0.54)
  local copies, waits for them, and re-layouts: 97.7 us -> 2.26 us
  Pallas kernels: 0 us -> 52.7 us
  matrix products: 44.5 us -> 0 us
  other arithmetic: 12.9 us -> 2.04 us
  starting transfers between devices: 17.9 us -> 26 us
  waiting for transfers between devices: 11.1 us -> 15.7 us
    pallas_call x0 -> x4, Pallas kernels: none -> 52.7 us  [the longest x1 15.9 us: points_stage(): pl.pallas_call(points_kernel, out_shape=(jax.ShapeDtypeStruct((PTS, 256),...]
    gather x3 -> x0, local copies, waits for them, and re-layouts: 49.5 us -> none  [the longest x1 18.5 us: local(): return jnp.take(result, inverse, axis=0)]
    dot_general x8 -> x0, matrix products: 44.5 us -> none  [the longest x1 18.7 us: local(): jnp.einsum('dnp,dnq->npq', grouped, grouped, precision=lax.Precision.HIGH...]
    scatter x1 -> x0, local copies, waits for them, and re-layouts: 15.5 us -> none  [local(): inverse = jnp.zeros((points,), jnp.int32).at[ordering].set(positions)]
    reshape x5 -> x0, local copies, waits for them, and re-layouts: 11.7 us -> none  [the longest x1 5.65 us: local(): result = jnp.einsum('npq,nqc->npc', kernel, values.reshape(leaves, LEAF,...]
    ppermute x6 -> x11, starting transfers between devices: 14.4 us -> 26 us  [the longest x7 18.7 us: swap(): return lax.ppermute(value, 'leaf', pairs)]
    another operation x5 -> x0, local copies, waits for them, and re-layouts: 6.96 us -> none  [the longest x2 3.13 us: local(): left_basis[crossing + inside - 1].reshape(RANK, node_count, node_size)]
    add x1 -> x0, local copies, waits for them, and re-layouts: 5.62 us -> none  [local(): result + jnp.einsum('rnm,nrc->nmc', left_part, sibling, preferred_element...]
  transfers between devices with their start and end apart: 7 -> 11, of which waited for: 2 -> 5; matrix products, arithmetic and copies ran while one was open for 48% -> 2% of each run, Pallas kernels for 0% -> 25%
where the time goes in v1:
time: 99.6 us; the launch traced here: 98.9 us
  Pallas kernels  52.7 us (53%)
  starting transfers between devices  26 us (26%)
  waiting for transfers between devices  15.7 us (16%)
  local copies, waits for them, and re-layouts  2.26 us (2%)
  other arithmetic  2.04 us (2%)
    ppermute x7, starting transfers between devices, swap(): return lax.ppermute(value, 'leaf', pairs)  18.7 us
    pallas_call x1, Pallas kernels, points_stage(): pl.pallas_call(points_kernel, out_shape=(jax.ShapeDtypeStruct((PTS, 256),...  15.9 us
    ppermute x7, waiting for transfers between devices, swap(): return lax.ppermute(value, 'leaf', pairs)  15.7 us
    pallas_call x1, Pallas kernels, finish_stage(): pl.pallas_call(finish_kernel, grid=(1,), out_shape=jax.ShapeDtypeStruct((...  14.2 us
    pallas_call x1, Pallas kernels, right_stage(): pl.pallas_call(right_kernel, out_shape=(jax.ShapeDtypeStruct((PTS, COLS),...  13.8 us
    pallas_call x1, Pallas kernels, near_stage(): pl.pallas_call(near_kernel, grid=(LEAVES,), out_shape=jax.ShapeDtypeStruc...  8.88 us
    ppermute x1, starting transfers between devices, local(): lax.ppermute(fifth, 'leaf', [(s, s ^ 1) for s in range(64) if s % 2 == 0])  3.05 us
  transfers between devices with their start and end apart: 11, of which 5 were waited for; matrix products, arithmetic and copies ran while one was open for 2% of the time, Pallas kernels for 25%

profile of v1, /device:TPU:0, one launch (start us, length us, event | category | flops | bytes accessed | tf_op | source)
XLA Modules:
  0.0 98.9 jit_solution(1588070414410267924)
XLA Ops:
  0.0 13.8 %right_stage.1 = (bf16[4096,256]{1,0:T(8,128)(2,1)}, f32[4,96,256]{2,1,0:T(8,128)}, f32[3,96,256]{2,1,0:T(8,128)}, bf16[2,96,256]{2,1,0:T(8,128)(2,1)}, bf16[4,96,256]{2,1,0:T(8,128)(2,1)}) custom-call(s32[4096]{0:T(1024)} %bitcast.15, s32[1]{0:T(128)} %bitcast.1.core, bf16[4096,256]{1,0:T(8,128)(2,1)} %probes.1, bf16[8,96,4096]{2,1,0:T(8,128)(2,1)} %right.1), custom_call_target="tpu_custom_call" | custom-call | flops 1610612736 | bytes 12582912 | tf_op jit(solution)/shard_map/right_stage/pallas_call | solution.py:100
  13.8 0.0 copy-start.2
  13.8 0.0 copy-start.6
  13.8 0.0 collective-permute-start.1
  13.9 1.9 %collective-permute-done.1 = f32[4,96,256]{2,1,0:T(8,128)S(1)} collective-permute-done((f32[4,96,256]{2,1,0:T(8,128)}, f32[4,96,256]{2,1,0:T(8,128)S(1)}, u32[]{:S(2)}, u32[]{:S(2)}) %collective-permute-start.1) | collective-permute-done | bytes 393248 | tf_op jit(solution)/shard_map/ppermute | solution.py:311
  15.8 1.0 %slice_add_fusion = f32[3,96,256]{2,1,0:T(8,128)S(1)} fusion(f32[3,96,256]{2,1,0:T(8,128)} %get-tuple-element.18, f32[4,96,256]{2,1,0:T(8,128)S(1)} %collective-permute-done.1), kind=kLoop, calls=%fused_computation | loop fusion | flops 73728 | bytes 884736 | tf_op jit(solution)/shard_map/add | solution.py:326
  16.8 0.7 collective-permute-start.3
  17.5 3.4 %collective-permute-start.2 = (f32[2,96,256]{2,1,0:T(8,128)S(1)}, f32[2,96,256]{2,1,0:T(8,128)S(1)}, u32[]{:S(2)}, u32[]{:S(2)}) collective-permute-start(f32[2,96,256]{2,1,0:T(8,128)S(1)} %slice.48), channel_id=1, source_target_pairs={{0,16},{2,6},{4,20},{6,2},{8,24},{10,14},{12,28},{14,10},{16,0},{1... | collective-permute-start | bytes 589832 | tf_op jit(solution)/shard_map/ppermute | solution.py:311
  20.9 0.0 collective-permute-done.3
  20.9 3.8 %collective-permute-done.2 = f32[2,96,256]{2,1,0:T(8,128)S(1)} collective-permute-done((f32[2,96,256]{2,1,0:T(8,128)S(1)}, f32[2,96,256]{2,1,0:T(8,128)S(1)}, u32[]{:S(2)}, u32[]{:S(2)}) %collective-permute-start.2) | collective-permute-done | bytes 196640 | tf_op jit(solution)/shard_map/ppermute | solution.py:311
  24.8 1.7 %collective-permute-start.4 = (f32[2,96,256]{2,1,0:T(8,128)S(1)}, f32[2,96,256]{2,1,0:T(8,128)S(1)}, u32[]{:S(2)}, u32[]{:S(2)}) collective-permute-start(f32[2,96,256]{2,1,0:T(8,128)S(1)} %maximum_select_fusion.1), channel_id=1, source_target_pairs={{0,4},{2,14},{4,0},{6,10},{8,12},{10,6},{12,8},{14,2},{16,20},{18,... | collective-permute-start | bytes 589832 | tf_op jit(solution)/shard_map/ppermute | solution.py:311
  26.5 4.1 %collective-permute-done.4 = f32[2,96,256]{2,1,0:T(8,128)S(1)} collective-permute-done((f32[2,96,256]{2,1,0:T(8,128)S(1)}, f32[2,96,256]{2,1,0:T(8,128)S(1)}, u32[]{:S(2)}, u32[]{:S(2)}) %collective-permute-start.4) | collective-permute-done | bytes 196640 | tf_op jit(solution)/shard_map/ppermute | solution.py:311
  30.6 3.0 %collective-permute-start.5 = (f32[2,96,256]{2,1,0:T(8,128)S(1)}, f32[2,96,256]{2,1,0:T(8,128)S(1)}, u32[]{:S(2)}, u32[]{:S(2)}) collective-permute-start(f32[2,96,256]{2,1,0:T(8,128)S(1)} %fusion.1), channel_id=1, source_target_pairs={{0,12},{2,18},{4,8},{6,22},{8,4},{10,26},{12,0},{14,30},{16,28},{1... | collective-permute-start | bytes 589832 | tf_op jit(solution)/shard_map/ppermute | solution.py:311
  33.6 4.0 %collective-permute-done.5 = f32[2,96,256]{2,1,0:T(8,128)S(1)} collective-permute-done((f32[2,96,256]{2,1,0:T(8,128)S(1)}, f32[2,96,256]{2,1,0:T(8,128)S(1)}, u32[]{:S(2)}, u32[]{:S(2)}) %collective-permute-start.5) | collective-permute-done | bytes 196640 | tf_op jit(solution)/shard_map/ppermute | solution.py:311
  37.6 3.9 %collective-permute-start.6 = (f32[2,96,256]{2,1,0:T(8,128)S(1)}, f32[2,96,256]{2,1,0:T(8,128)S(1)}, u32[]{:S(2)}, u32[]{:S(2)}) collective-permute-start(f32[2,96,256]{2,1,0:T(8,128)S(1)} %add.30), channel_id=1, source_target_pairs={{0,32},{4,36},{8,40},{12,44},{16,48},{20,52},{24,56},{28,60},{32,0... | collective-permute-start | bytes 589832 | tf_op jit(solution)/shard_map/ppermute | solution.py:311
  41.6 0.0 copy-done.2
  41.6 0.0 copy-done.6
  41.6 0.1 broadcast_divide_fusion.own
  41.7 0.0 copy-start
  41.7 1.7 %collective-permute-start = (f32[32,4096]{1,0:T(8,128)S(1)}, f32[32,4096]{1,0:T(8,128)S(1)}, u32[]{:S(2)}, u32[]{:S(2)}) collective-permute-start(f32[32,4096]{1,0:T(8,128)S(1)} %broadcast_divide_fusion.own), channel_id=1, source_target_pairs={{0,1},{1,0},{2,3},{3,2},{4,5},{5,4},{6,7},{7,6},{8,9},{9,8},{10,11... | collective-permute-start | bytes 1572872 | tf_op jit(solution)/shard_map/ppermute | solution.py:322
  43.4 1.8 %collective-permute-done.6 = f32[2,96,256]{2,1,0:T(8,128)S(1)} collective-permute-done((f32[2,96,256]{2,1,0:T(8,128)S(1)}, f32[2,96,256]{2,1,0:T(8,128)S(1)}, u32[]{:S(2)}, u32[]{:S(2)}) %collective-permute-start.6) | collective-permute-done | bytes 196640 | tf_op jit(solution)/shard_map/ppermute | solution.py:311
  45.2 6.0 %collective-permute-start.7 = (f32[96,256]{1,0:T(8,128)S(1)}, f32[96,256]{1,0:T(8,128)S(1)}, u32[]{:S(2)}, u32[]{:S(2)}) collective-permute-start(f32[96,256]{1,0:T(8,128)S(1)} %get-tuple-element.22), channel_id=1, source_target_pairs={{0,96},{4,100},{8,104},{12,108},{16,112},{20,116},{24,120},{28,124... | collective-permute-start | bytes 294920 | tf_op jit(solution)/shard_map/ppermute | solution.py:311
  51.3 0.6 slice_bitcast_fusion.1.zero
  51.9 0.0 collective-permute-done.other
  51.9 0.0 copy-done
  51.9 0.0 copy-start.1
  51.9 0.8 copy-done.1
  52.7 15.9 %points_stage.1 = (bf16[4096,256]{1,0:T(8,128)(2,1)}, bf16[4096,256]{1,0:T(8,128)(2,1)}) custom-call(s32[4096]{0:T(1024)} %bitcast.16, f32[32,4096]{1,0:T(8,128)} %copy-done, f32[32,4096]{1,0:T(8,128)} %copy-done.1), custom_call_target="tpu_custom_call" | custom-call | flops 16777216 | bytes 5242880 | tf_op jit(solution)/shard_map/points_stage/pallas_call | solution.py:168
  68.7 1.3 %collective-permute-start.9 = (f32[96,256]{1,0:T(8,128)S(1)}, f32[96,256]{1,0:T(8,128)S(1)}, u32[]{:S(2)}, u32[]{:S(2)}) collective-permute-start(f32[96,256]{1,0:T(8,128)S(1)} %get-tuple-element.21), channel_id=1, source_target_pairs={{0,2},{4,6},{8,10},{12,14},{16,18},{20,22},{24,26},{28,30},{32,34}... | collective-permute-start | bytes 294920 | tf_op jit(solution)/shard_map/ppermute | solution.py:344
  70.0 0.0 collective-permute-done.7
  70.0 0.8 pad_maximum_fusion
  70.7 1.3 %collective-permute-start.8 = (f32[3,96,256]{2,1,0:T(8,128)S(1)}, f32[3,96,256]{2,1,0:T(8,128)S(1)}, u32[]{:S(2)}, u32[]{:S(2)}) collective-permute-start(f32[3,96,256]{2,1,0:T(8,128)S(1)} %get-tuple-element.19), channel_id=1, source_target_pairs={{2,0},{6,4},{10,8},{14,12},{18,16},{22,20},{26,24},{30,28},{34,32}... | collective-permute-start | bytes 884744 | tf_op jit(solution)/shard_map/ppermute | solution.py:343
  72.0 3.0 %collective-permute-start.10 = (f32[96,256]{1,0:T(8,128)S(1)}, f32[96,256]{1,0:T(8,128)S(1)}, u32[]{:S(2)}, u32[]{:S(2)}) collective-permute-start(f32[96,256]{1,0:T(8,128)S(1)} %collective-permute-done.7), channel_id=1, source_target_pairs={{0,2},{4,6},{8,10},{12,14},{16,18},{20,22},{24,26},{28,30},{32,34}... | collective-permute-start | bytes 294920 | tf_op jit(solution)/shard_map/ppermute | solution.py:345
  75.1 8.9 %near_stage.1.near = f32[4096,256]{1,0:T(8,128)} custom-call(bf16[4096,256]{1,0:T(8,128)(2,1)} %get-tuple-element.12.left, bf16[4096,256]{1,0:T(8,128)(2,1)} %get-tuple-element.13.right, bf16[4096,256]{1,0:T(8,128)(2,1)} %get-tuple-element.14.values, bf16[8,96,4096]{2,1,0:T(8,128)(2,1)} %basis.3, bf16[2,96,256]{2,1,0:T(8,128)(2,1)} %get-tuple-element.15.coef7, ...), custom_call_target="tpu_custom_call" | custom-call | flops 4294967296 | bytes 12582912 | tf_op jit(solution)/shard_map/near_stage/pallas_call | solution.py:208
  84.0 0.0 collective-permute-done.9.fourth
  84.0 0.0 copy-start.4
  84.0 0.0 collective-permute-done.10.fifth
  84.0 0.0 copy-start.5
  84.0 0.0 collective-permute-done.8.theirs
  84.0 0.0 copy-start.3
  84.0 0.6 copy-done.4
  84.6 0.1 copy-done.5
  84.7 0.1 copy-done.3
  84.8 14.2 %finish_stage.1 = f32[4096,256]{1,0:T(8,128)} custom-call(s32[4096]{0:T(1024)} %bitcast.17, s32[1]{0:T(128)} %bitcast.1.core, f32[4096,256]{1,0:T(8,128)} %near_stage.1.near, bf16[8,96,4096]{2,1,0:T(8,128)(2,1)} %basis.3, f32[96,256]{1,0:T(8,128)} %slice_bitcast_fusion.1.zero, f32[3,96,256]{2,1,0:T(8,128)} %get-tuple-element.20.mine, ...), custom_call_target="tpu_custom_call" | custom-call | flops 1207959552 | bytes 16777216 | tf_op jit(solution)/shard_map/finish_stage/pallas_call | solution.py:276
  (12 shorter events, 0.2 us)
Async XLA Ops:
  13.8 27.8 %copy-start.2 = (f32[32,4096]{1,0:T(8,128)S(1)}, f32[32,4096]{1,0:T(8,128)}, u32[]{:S(2)}) copy-start(f32[32,4096]{1,0:T(8,128)} %param.6) | copy-start | bytes 1572868
  13.8 27.8 %copy-start.6 = (f32[32]{0:T(128)S(1)}, f32[32]{0:T(128)}, u32[]{:S(2)}) copy-start(f32[32]{0:T(128)} %param.7) | copy-start | bytes 388
  13.8 2.0 %collective-permute-start.1 = (f32[4,96,256]{2,1,0:T(8,128)}, f32[4,96,256]{2,1,0:T(8,128)S(1)}, u32[]{:S(2)}, u32[]{:S(2)}) collective-permute-start(f32[4,96,256]{2,1,0:T(8,128)} %get-tuple-element.17), channel_id=1, source_target_pairs={{0,2},{2,0},{4,6},{6,4},{8,10},{10,8},{12,14},{14,12},{16,18},{18,... | collective-permute-start | bytes 1179656 | tf_op jit(solution)/shard_map/ppermute | solution.py:311
  16.8 4.1 %collective-permute-start.3 = (f32[96,256]{1,0:T(8,128)S(1)}, f32[96,256]{1,0:T(8,128)S(1)}, u32[]{:S(2)}, u32[]{:S(2)}) collective-permute-start(f32[96,256]{1,0:T(8,128)S(1)} %slice_bitcast_fusion), channel_id=1, source_target_pairs={{2,6},{6,2},{10,14},{14,10},{18,22},{22,18},{26,30},{30,26},{34,38... | collective-permute-start | bytes 294920 | tf_op jit(solution)/shard_map/ppermute | solution.py:311
  17.5 7.3 %collective-permute-start.2 = (f32[2,96,256]{2,1,0:T(8,128)S(1)}, f32[2,96,256]{2,1,0:T(8,128)S(1)}, u32[]{:S(2)}, u32[]{:S(2)}) collective-permute-start(f32[2,96,256]{2,1,0:T(8,128)S(1)} %slice.48), channel_id=1, source_target_pairs={{0,16},{2,6},{4,20},{6,2},{8,24},{10,14},{12,28},{14,10},{16,0},{1... | collective-permute-start | bytes 589832 | tf_op jit(solution)/shard_map/ppermute | solution.py:311
  24.8 5.7 %collective-permute-start.4 = (f32[2,96,256]{2,1,0:T(8,128)S(1)}, f32[2,96,256]{2,1,0:T(8,128)S(1)}, u32[]{:S(2)}, u32[]{:S(2)}) collective-permute-start(f32[2,96,256]{2,1,0:T(8,128)S(1)} %maximum_select_fusion.1), channel_id=1, source_target_pairs={{0,4},{2,14},{4,0},{6,10},{8,12},{10,6},{12,8},{14,2},{16,20},{18,... | collective-permute-start | bytes 589832 | tf_op jit(solution)/shard_map/ppermute | solution.py:311
  30.6 7.0 %collective-permute-start.5 = (f32[2,96,256]{2,1,0:T(8,128)S(1)}, f32[2,96,256]{2,1,0:T(8,128)S(1)}, u32[]{:S(2)}, u32[]{:S(2)}) collective-permute-start(f32[2,96,256]{2,1,0:T(8,128)S(1)} %fusion.1), channel_id=1, source_target_pairs={{0,12},{2,18},{4,8},{6,22},{8,4},{10,26},{12,0},{14,30},{16,28},{1... | collective-permute-start | bytes 589832 | tf_op jit(solution)/shard_map/ppermute | solution.py:311
  37.6 7.6 %collective-permute-start.6 = (f32[2,96,256]{2,1,0:T(8,128)S(1)}, f32[2,96,256]{2,1,0:T(8,128)S(1)}, u32[]{:S(2)}, u32[]{:S(2)}) collective-permute-start(f32[2,96,256]{2,1,0:T(8,128)S(1)} %add.30), channel_id=1, source_target_pairs={{0,32},{4,36},{8,40},{12,44},{16,48},{20,52},{24,56},{28,60},{32,0... | collective-permute-start | bytes 589832 | tf_op jit(solution)/shard_map/ppermute | solution.py:311
  41.7 10.2 %copy-start = (f32[32,4096]{1,0:T(8,128)}, f32[32,4096]{1,0:T(8,128)S(1)}, u32[]{:S(2)}) copy-start(f32[32,4096]{1,0:T(8,128)S(1)} %broadcast_divide_fusion.own) | copy-start | bytes 1572868
  41.7 10.2 %collective-permute-start = (f32[32,4096]{1,0:T(8,128)S(1)}, f32[32,4096]{1,0:T(8,128)S(1)}, u32[]{:S(2)}, u32[]{:S(2)}) collective-permute-start(f32[32,4096]{1,0:T(8,128)S(1)} %broadcast_divide_fusion.own), channel_id=1, source_target_pairs={{0,1},{1,0},{2,3},{3,2},{4,5},{5,4},{6,7},{7,6},{8,9},{9,8},{10,11... | collective-permute-start | bytes 1572872 | tf_op jit(solution)/shard_map/ppermute | solution.py:322
  45.2 24.7 %collective-permute-start.7 = (f32[96,256]{1,0:T(8,128)S(1)}, f32[96,256]{1,0:T(8,128)S(1)}, u32[]{:S(2)}, u32[]{:S(2)}) collective-permute-start(f32[96,256]{1,0:T(8,128)S(1)} %get-tuple-element.22), channel_id=1, source_target_pairs={{0,96},{4,100},{8,104},{12,108},{16,112},{20,116},{24,120},{28,124... | collective-permute-start | bytes 294920 | tf_op jit(solution)/shard_map/ppermute | solution.py:311
  51.9 0.8 copy-start.1
  68.7 15.3 %collective-permute-start.9 = (f32[96,256]{1,0:T(8,128)S(1)}, f32[96,256]{1,0:T(8,128)S(1)}, u32[]{:S(2)}, u32[]{:S(2)}) collective-permute-start(f32[96,256]{1,0:T(8,128)S(1)} %get-tuple-element.21), channel_id=1, source_target_pairs={{0,2},{4,6},{8,10},{12,14},{16,18},{20,22},{24,26},{28,30},{32,34}... | collective-permute-start | bytes 294920 | tf_op jit(solution)/shard_map/ppermute | solution.py:344
  70.7 13.3 %collective-permute-start.8 = (f32[3,96,256]{2,1,0:T(8,128)S(1)}, f32[3,96,256]{2,1,0:T(8,128)S(1)}, u32[]{:S(2)}, u32[]{:S(2)}) collective-permute-start(f32[3,96,256]{2,1,0:T(8,128)S(1)} %get-tuple-element.19), channel_id=1, source_target_pairs={{2,0},{6,4},{10,8},{14,12},{18,16},{22,20},{26,24},{30,28},{34,32}... | collective-permute-start | bytes 884744 | tf_op jit(solution)/shard_map/ppermute | solution.py:343
  72.0 12.0 %collective-permute-start.10 = (f32[96,256]{1,0:T(8,128)S(1)}, f32[96,256]{1,0:T(8,128)S(1)}, u32[]{:S(2)}, u32[]{:S(2)}) collective-permute-start(f32[96,256]{1,0:T(8,128)S(1)} %collective-permute-done.7), channel_id=1, source_target_pairs={{0,2},{4,6},{8,10},{12,14},{16,18},{20,22},{24,26},{28,30},{32,34}... | collective-permute-start | bytes 294920 | tf_op jit(solution)/shard_map/ppermute | solution.py:345
  84.0 0.6 copy-start.4
  84.0 0.7 copy-start.5
  84.0 0.8 copy-start.3

commit v2 on v0

v2 whole, which is shorter than its diff:
```python
import functools
import math

import jax
import jax.numpy as jnp
from jax import lax
from jax.experimental import pallas as pl
from jax.experimental.pallas import tpu as pltpu
from jax.sharding import PartitionSpec as P


DIM = 64
RANK = 96
LEAF = 1024
CROSS = 6
PTS = 4096
COLS = 256
LEAVES = PTS // LEAF
BLOCK = 256
BLOCKS = PTS // BLOCK
ROOT = math.sqrt(math.log2(math.e))
F32 = jnp.float32
BF16 = jnp.bfloat16
LIMIT = 30 * 1024 * 1024
FULL = 60500 * 1024
HALF = RANK // 2
HBM = pl.BlockSpec(memory_space=pltpu.HBM)
VMEM = pl.BlockSpec(memory_space=pltpu.VMEM)
SMEM = pl.BlockSpec(memory_space=pltpu.SMEM)


def call(body, outs, ins, scratch, flops, moved, exps=0, limit=LIMIT):
    return pl.pallas_call(
        body,
        out_shape=tuple(jax.ShapeDtypeStruct(shape, kind) for shape, kind, _ in outs),
        in_specs=ins,
        out_specs=tuple(space for _, _, space in outs),
        scratch_shapes=scratch,
        compiler_params=pltpu.CompilerParams(vmem_limit_bytes=limit),
        cost_estimate=pl.CostEstimate(flops=flops, bytes_accessed=moved, transcendentals=exps),
    )


def right_kernel(order, core, probes, right, values, send, keep, double,
                 raw, table, source, basis, rows, moved, acc, sems):
    get_order = pltpu.make_async_copy(order, raw, sems.at[0])
    get_order.start()
    get_probes = []
    for part in range(4):
        span = pl.ds(part * LEAF, LEAF)
        get_probes.append(pltpu.make_async_copy(probes.at[span], source.at[span], sems.at[1 + part]))
        get_probes[-1].start()
    get_right = []
    for part in range(4):
        span = pl.ds(part * LEAF, LEAF)
        get_right.append(
            pltpu.make_async_copy(
                right.at[pl.ds(0, CROSS), :, span], basis.at[:, :, span], sems.at[5 + part]
            )
        )
        get_right[-1].start()
    get_order.wait()
    double[...] = raw[...] * 2
    get_table = pltpu.make_async_copy(double, table, sems.at[9])
    get_table.start()

    def spread(step, carry):
        base = pl.multiple_of(step * 16, 16)
        block = source[pl.ds(base, 16), :].astype(F32)
        rows[pl.ds(2 * base, 16, stride=2), :] = block[:, :128]
        rows[pl.ds(2 * base + 1, 16, stride=2), :] = block[:, 128:]
        return carry

    for part in range(4):
        get_probes[part].wait()
        lax.fori_loop(part * 64, part * 64 + 64, spread, 0, unroll=8)
    get_table.wait()
    for k in range(PTS):
        moved[pl.ds(2 * k, 2), :] = rows[pl.ds(table[k // 128, k % 128], 2), :]

    def gather_back(step, carry):
        base = pl.multiple_of(step * 64, 64)
        low = moved[pl.ds(2 * base, 64, stride=2), :]
        high = moved[pl.ds(2 * base + 1, 64, stride=2), :]
        values[pl.ds(base, 64), :] = jnp.concatenate([low, high], axis=1).astype(BF16)
        return carry

    lax.fori_loop(0, PTS // 64, gather_back, 0, unroll=4)
    for leaf in range(LEAVES):
        get_right[leaf].wait()
        span = pl.ds(leaf * LEAF, LEAF)
        part = jnp.dot(
            basis[:, :, span].reshape(CROSS * RANK, LEAF), values[span, :], preferred_element_type=F32
        )
        if leaf == 0:
            acc[...] = part
        else:
            acc[...] += part
    send[pl.ds(0, RANK), :] = acc[pl.ds((CROSS - 1) * RANK, RANK), :]
    for bit in range(1, CROSS):
        top = (CROSS - 1 - bit) * RANK
        mine = pl.multiple_of(top + core[0] * HALF, HALF)
        other = pl.multiple_of(top + (1 - core[0]) * HALF, HALF)
        keep[pl.ds((bit - 1) * HALF, HALF), :] = acc[pl.ds(mine, HALF), :]
        send[pl.ds(RANK + (bit - 1) * HALF, HALF), :] = acc[pl.ds(other, HALF), :]


def right_stage(order, core, probes, right):
    return call(
        right_kernel,
        [
            ((PTS, COLS), BF16, VMEM),
            ((RANK + 5 * HALF, COLS), F32, VMEM),
            ((5 * HALF, COLS), F32, VMEM),
            ((32, 128), jnp.int32, VMEM),
        ],
        [HBM, SMEM, HBM, HBM],
        [
            pltpu.VMEM((32, 128), jnp.int32),
            pltpu.SMEM((32, 128), jnp.int32),
            pltpu.VMEM((PTS, COLS), BF16),
            pltpu.VMEM((CROSS, RANK, PTS), BF16),
            pltpu.VMEM((2 * PTS, 128), F32),
            pltpu.VMEM((2 * PTS, 128), F32),
            pltpu.VMEM((CROSS * RANK, COLS), F32),
            pltpu.SemaphoreType.DMA((10,)),
        ],
        2 * 576 * PTS * COLS, 12 << 20, limit=FULL,
    )(order, core, probes, right)


def coef_kernel(right, values, coef7, coef8):
    half = []
    for leaf in range(LEAVES):
        span = pl.ds(leaf * LEAF, LEAF)
        part = jnp.dot(
            right[:, :, span].reshape(2 * RANK, LEAF), values[span, :], preferred_element_type=F32
        )
        coef8[leaf] = (part[RANK:] * (1.0 / math.sqrt(LEAF))).astype(BF16)
        half.append(part[:RANK])
    for node in range(2):
        total = half[2 * node] + half[2 * node + 1]
        coef7[node] = (total * (1.0 / math.sqrt(2 * LEAF))).astype(BF16)


def coef_stage(right, values):
    return call(
        coef_kernel,
        [((2, RANK, COLS), BF16, VMEM), ((4, RANK, COLS), BF16, VMEM)],
        [VMEM, VMEM],
        [],
        2 * 192 * PTS * COLS, 4 << 20,
    )(right, values)


def turn_kernel(own, other, rows):
    line = lax.broadcasted_iota(jnp.int32, (DIM, 128), 0)
    for step in range(PTS // 128):
        span = pl.ds(step * 128, 128)
        tile = jnp.concatenate([own[:, span], other[:, span]], axis=0) * ROOT
        norm = jnp.sum(tile * tile, axis=0, keepdims=True) * -0.5
        first = norm.astype(BF16).astype(F32)
        second = (norm - first).astype(BF16).astype(F32)
        third = norm - first - second
        early = jnp.where(line == 0, first, jnp.where(line == 1, second, third))
        late = jnp.where(line == 3, first, jnp.where(line == 4, second, third))
        extra_left = jnp.where(line < 3, early, jnp.where(line < 6, 1.0, 0.0))
        extra_right = jnp.where(line < 3, 1.0, jnp.where(line < 6, late, 0.0))
        rows[pl.ds(2 * step * 128, 128, stride=2), :] = jnp.concatenate([tile, tile], axis=0).T
        rows[pl.ds(2 * step * 128 + 1, 128, stride=2), :] = jnp.concatenate(
            [extra_right, extra_left], axis=0
        ).T


def turn_stage(own, other):
    return call(
        turn_kernel,
        [((2 * PTS, 128), F32, VMEM)],
        [VMEM, VMEM],
        [],
        PTS * 64, 5 << 20,
    )(own, other)[0]


def points_kernel(half, order, rows, left, right, moved):
    count = BLOCKS // 2

    def gather(block, carry):
        base = pl.multiple_of(block * (2 * BLOCK), 2 * BLOCK)
        for k in range(BLOCK):
            take = order[2 * (block + half * count) + k // 128, k % 128]
            moved[pl.ds(base + 2 * k, 2), :] = rows[pl.ds(take, 2), :]
        return carry

    def split(step, carry):
        base = pl.multiple_of(step * 64, 64)
        span = pl.ds(base, 64)
        x = moved[pl.ds(2 * base, 64, stride=2), :]
        extra = moved[pl.ds(2 * base + 1, 64, stride=2), :]
        front = lax.broadcasted_iota(jnp.int32, x.shape, 1) < DIM
        high = x.astype(BF16).astype(F32)
        low = x - high
        left[span, :] = jnp.concatenate([high, jnp.where(front, low, extra)], axis=1).astype(BF16)
        right[span, :] = jnp.concatenate(
            [jnp.where(front, high, low), jnp.where(front, high, pltpu.roll(extra, DIM, 1))], axis=1
        ).astype(BF16)
        return carry

    lax.fori_loop(0, count, gather, 0)
    lax.fori_loop(0, PTS // 128, split, 0, unroll=2)


def points_stage(half, order, rows):
    return call(
        functools.partial(points_kernel, half),
        [((PTS // 2, 256), BF16, VMEM), ((PTS // 2, 256), BF16, VMEM)],
        [SMEM, VMEM],
        [pltpu.VMEM((PTS, 128), F32)],
        PTS * 2048, 4 << 20,
    )(order, rows)


def near_kernel(leaf, left, right, values, basis, coef7, coef8, near):
    coef = jnp.concatenate([coef7[1 - leaf // 2], coef8[leaf ^ 1]], axis=0)
    local = pl.ds((leaf % 2) * LEAF, LEAF)
    for step in range(LEAF // BLOCK):
        span = pl.ds(step * BLOCK, BLOCK)
        power = lax.dot_general(
            left[pl.ds((leaf % 2) * LEAF + step * BLOCK, BLOCK), :],
            right[local, :],
            (((1,), (1,)), ((), ())),
            preferred_element_type=F32,
        )
        kernel = jnp.exp2(power).astype(BF16)
        total = jnp.dot(kernel, values[pl.ds(leaf * LEAF, LEAF), :], preferred_element_type=F32)
        total += lax.dot_general(
            basis[CROSS:, :, pl.ds(leaf * LEAF + step * BLOCK, BLOCK)].reshape(2 * RANK, BLOCK),
            coef,
            (((0,), (0,)), ((), ())),
            preferred_element_type=F32,
        )
        near[span, :] = total


def near_stage(leaf, left, right, values, basis, coef7, coef8):
    return call(
        functools.partial(near_kernel, leaf),
        [((LEAF, COLS), F32, VMEM)],
        [VMEM] * 6,
        [],
        2 * LEAF * LEAF * 512, 3 << 20, LEAF * LEAF,
    )(left, right, values, basis, coef7, coef8)[0]


def finish_kernel(order, core, near0, near1, near2, near3, basis, zero, first, second, third, fourth,
                  fifth, others, last, out, coef, low, high, moved_low, moved_high, sems):
    root = [1.0 / math.sqrt(PTS * 2**bit) for bit in range(CROSS)]
    near = [near0, near1, near2, near3]
    mine = [first, second, third, fourth, fifth]

    def put(bit, start, value):
        begin = pl.multiple_of((CROSS - 1 - bit) * RANK + start, 16)
        coef[pl.ds(begin, value.shape[0]), :] = (value * root[bit]).astype(BF16)

    put(0, 0, zero[:RANK])
    for bit in range(1, CROSS):
        put(bit, core[0] * HALF, mine[bit - 1][:HALF])
        other = last[...] if bit == 5 else others[pl.ds((bit - 1) * HALF, HALF), :]
        put(bit, (1 - core[0]) * HALF, other)

    for block in range(BLOCKS):
        leaf, step = divmod(block, LEAF // BLOCK)
        span = pl.ds(block * BLOCK, BLOCK)
        total = near[leaf][pl.ds(step * BLOCK, BLOCK), :] + lax.dot_general(
            basis[:CROSS, :, span].reshape(CROSS * RANK, BLOCK),
            coef[...],
            (((0,), (0,)), ((), ())),
            preferred_element_type=F32,
        )
        low[span, :] = total[:, :128]
        high[span, :] = total[:, 128:]

    def scatter(block, carry):
        base = pl.multiple_of(block * 128, 128)
        for k in range(128):
            to = pl.ds(order[block, k], 1)
            moved_low[to, :] = low[pl.ds(base + k, 1), :]
            moved_high[to, :] = high[pl.ds(base + k, 1), :]
        return carry

    lax.fori_loop(0, PTS // 128, scatter, 0)
    copies = []
    for part in range(2):
        moved = (moved_low, moved_high)[part]
        copies.append(
            pltpu.make_async_copy(moved.reshape(PTS // 8, 8, 128), out.at[:, part], sems.at[part])
        )
        copies[-1].start()
    for copy in copies:
        copy.wait()


def finish_stage(order, core, near, basis, coefs):
    out = call(
        finish_kernel,
        [((PTS // 8, 2, 8, 128), F32, HBM)],
        [SMEM, SMEM] + [VMEM] * 13,
        [pltpu.VMEM((CROSS * RANK, COLS), BF16)]
        + [pltpu.VMEM((PTS, 128), F32)] * 4
        + [pltpu.SemaphoreType.DMA((2,))],
        2 * 576 * PTS * COLS, 16 << 20,
    )(order, core, *near, basis, *coefs)[0]
    return out.transpose(0, 2, 1, 3).reshape(PTS, COLS)


CORE, XA, X2, YB, ZA, Z2 = 1, 2, 4, 8, 16, 32


def swap(value, mask):
    pairs = [(source, source ^ mask) for source in range(64)]
    return lax.ppermute(value, "leaf", pairs)


def body(coordinates, lengthscale, tree_order, probes, left_basis, right_basis):
    core = (lax.axis_index("leaf") % 2).reshape(1)
    order = tree_order.reshape(32, 128)
    scaled = coordinates / lengthscale[:, None]
    other = lax.ppermute(scaled, "cols", [(0, 1), (1, 0)])
    values, send, keep, double = right_stage(order, core, probes, right_basis)
    zero = swap(send, CORE)
    total = keep + zero[RANK:]
    first = swap(total, XA)
    total = total[HALF:] + first[HALF:]
    second = swap(total, X2)
    total = total[HALF:] + second[HALF:]
    third = swap(total, YB)
    total = total[HALF:] + third[HALF:]
    fourth = swap(total, ZA)
    total = total[HALF:] + fourth[HALF:]
    fifth = swap(total, Z2)
    ready = jnp.concatenate([first[:HALF], second[:HALF], third[:HALF], fourth[:HALF]])
    others = swap(ready, CORE)
    last = swap(fifth, CORE)
    coef7, coef8 = coef_stage(right_basis[CROSS:], values)
    rows = turn_stage(scaled, other)
    near = []
    for half in range(2):
        left, right = points_stage(half, double, rows)
        for leaf in (2 * half, 2 * half + 1):
            near.append(near_stage(leaf, left, right, values, left_basis, coef7, coef8))
    coefs = (zero, first, second, third, fourth, fifth, others, last)
    return finish_stage(order, core, near, left_basis, coefs)


def solution(mesh):
    placed = (
        P("cols", "leaf"),
        P("cols"),
        P("leaf", None),
        P("leaf", "cols"),
        P(None, None, "leaf"),
        P(None, None, "leaf"),
    )
    return jax.shard_map(
        body, mesh=mesh, in_specs=placed, out_specs=P("leaf", "cols"), check_vma=False
    )
```

time: 185 us -> 65.8 us (0.36)
  local copies, waits for them, and re-layouts: 97.7 us -> 1.56 us
  matrix products: 44.5 us -> 0 us
  Pallas kernels: 0 us -> 32.2 us
  other arithmetic: 12.9 us -> 1.17 us
    gather x3 -> x0, local copies, waits for them, and re-layouts: 49.5 us -> none  [the longest x1 18.5 us: local(): return jnp.take(result, inverse, axis=0)]
    dot_general x8 -> x0, matrix products: 44.5 us -> none  [the longest x1 18.7 us: local(): jnp.einsum('dnp,dnq->npq', grouped, grouped, precision=lax.Precision.HIGH...]
    pallas_call x0 -> x10, Pallas kernels: none -> 32.2 us  [the longest x1 9.17 us: finish_stage(): call(finish_kernel, [((PTS // 8, 2, 8, 128), F32, HBM)], [SMEM, SMEM] + [...]
    scatter x1 -> x0, local copies, waits for them, and re-layouts: 15.5 us -> none  [local(): inverse = jnp.zeros((points,), jnp.int32).at[ordering].set(positions)]
    reshape x5 -> x0, local copies, waits for them, and re-layouts: 11.7 us -> none  [the longest x1 5.65 us: local(): result = jnp.einsum('npq,nqc->npc', kernel, values.reshape(leaves, LEAF,...]
    another operation x5 -> x0, local copies, waits for them, and re-layouts: 6.96 us -> none  [the longest x2 3.13 us: local(): left_basis[crossing + inside - 1].reshape(RANK, node_count, node_size)]
    add x1 -> x0, local copies, waits for them, and re-layouts: 5.62 us -> none  [local(): result + jnp.einsum('rnm,nrc->nmc', left_part, sibling, preferred_element...]
    select_n x2 -> x0, other arithmetic: 4.83 us -> none  [the longest x1 3.94 us: local(): return jnp.take(result, inverse, axis=0)]
  transfers between devices with their start and end apart: 7 -> 9, of which waited for: 2 -> 5; matrix products, arithmetic and copies ran while one was open for 48% -> 3% of each run, Pallas kernels for 0% -> 24%
where the time goes in v2:
time: 65.8 us; the launch traced here: 64.5 us
  Pallas kernels  32.2 us (49%)
  starting transfers between devices  16.7 us (25%)
  waiting for transfers between devices  12.4 us (19%)
  local copies, waits for them, and re-layouts  1.56 us (2%)
  other arithmetic  1.17 us (2%)
    ppermute x8, starting transfers between devices, swap(): return lax.ppermute(value, 'leaf', pairs)  15 us
    ppermute x8, waiting for transfers between devices, swap(): return lax.ppermute(value, 'leaf', pairs)  12.4 us
    pallas_call x1, Pallas kernels, finish_stage(): call(finish_kernel, [((PTS // 8, 2, 8, 128), F32, HBM)], [SMEM, SMEM] + [...  9.17 us
    pallas_call x1, Pallas kernels, right_stage(): call(right_kernel, [((PTS, COLS), BF16, VMEM), ((RANK + 5 * HALF, COLS),...  7.9 us
    pallas_call x2, Pallas kernels, points_stage(): call(functools.partial(points_kernel, half), [((PTS // 2, 256), BF16, VME...  7.58 us
    pallas_call x4, Pallas kernels, near_stage(): call(functools.partial(near_kernel, leaf), [((LEAF, COLS), F32, VMEM)], [...  5.84 us
    ppermute x1, starting transfers between devices, body(): other = lax.ppermute(scaled, 'cols', [(0, 1), (1, 0)])  1.65 us
    slice x1, local copies, waits for them, and re-layouts, body(): coef7, coef8 = coef_stage(right_basis[CROSS:], values)  1.51 us
  transfers between devices with their start and end apart: 9, of which 5 were waited for; matrix products, arithmetic and copies ran while one was open for 3% of the time, Pallas kernels for 24%

profile of v2, /device:TPU:0, one launch (start us, length us, event | category | flops | bytes accessed | tf_op | source)
XLA Modules:
  0.0 64.5 jit_solution(16333530067965326459)
XLA Ops:
  0.0 0.0 copy-start.3
  0.0 0.0 copy-start.4
  0.0 7.9 %shard_map.64 = (bf16[4096,256]{1,0:T(8,128)(2,1)}, f32[336,256]{1,0:T(8,128)}, f32[240,256]{1,0:T(8,128)}, s32[32,128]{1,0:T(8,128)}) custom-call(s32[32,128]{1,0:T(8,128)} %bitcast.7, s32[1]{0:T(128)} %bitcast.1.core, bf16[4096,256]{1,0:T(8,128)(2,1)} %probes.1, bf16[8,96,4096]{2,1,0:T(8,128)(2,1)} %right.1), custom_call_target="tpu_custom_call" | custom-call | flops 1207959552 | bytes 12582912 | tf_op jit(solution)/shard_map/pallas_call | solution.py:109
  7.9 0.0 copy-start
  7.9 0.1 collective-permute-start.1
  8.0 1.9 %collective-permute-done.1.zero = f32[336,256]{1,0:T(8,128)S(1)} collective-permute-done((f32[336,256]{1,0:T(8,128)}, f32[336,256]{1,0:T(8,128)S(1)}, u32[]{:S(2)}, u32[]{:S(2)}) %collective-permute-start.1) | collective-permute-done | bytes 344096 | tf_op jit(solution)/shard_map/ppermute | solution.py:321
  9.9 1.0 %slice_add_fusion = f32[240,256]{1,0:T(8,128)S(1)} fusion(f32[240,256]{1,0:T(8,128)} %get-tuple-element.24, f32[336,256]{1,0:T(8,128)S(1)} %collective-permute-done.1.zero), kind=kLoop, calls=%fused_computation.1 | loop fusion | flops 61440 | bytes 737280 | tf_op jit(solution)/shard_map/add | solution.py:331
  10.8 1.7 %collective-permute-start.2 = (f32[240,256]{1,0:T(8,128)S(1)}, f32[240,256]{1,0:T(8,128)S(1)}, u32[]{:S(2)}, u32[]{:S(2)}) collective-permute-start(f32[240,256]{1,0:T(8,128)S(1)} %slice_add_fusion), channel_id=1, source_target_pairs={{0,4},{2,6},{4,0},{6,2},{8,12},{10,14},{12,8},{14,10},{16,20},{18,... | collective-permute-start | bytes 737288 | tf_op jit(solution)/shard_map/ppermute | solution.py:321
  12.5 0.0 copy-done.3
  12.5 0.0 copy-done.4
  12.5 0.1 broadcast_divide_fusion.own
  12.6 1.7 %collective-permute-start = (f32[32,4096]{1,0:T(8,128)S(1)}, f32[32,4096]{1,0:T(8,128)S(1)}, u32[]{:S(2)}, u32[]{:S(2)}) collective-permute-start(f32[32,4096]{1,0:T(8,128)S(1)} %broadcast_divide_fusion.own), channel_id=1, source_target_pairs={{0,1},{1,0},{2,3},{3,2},{4,5},{5,4},{6,7},{7,6},{8,9},{9,8},{10,11... | collective-permute-start | bytes 1572872 | tf_op jit(solution)/shard_map/ppermute | solution.py:328
  14.3 4.6 %collective-permute-done.2.first = f32[240,256]{1,0:T(8,128)S(1)} collective-permute-done((f32[240,256]{1,0:T(8,128)S(1)}, f32[240,256]{1,0:T(8,128)S(1)}, u32[]{:S(2)}, u32[]{:S(2)}) %collective-permute-start.2) | collective-permute-done | bytes 245792 | tf_op jit(solution)/shard_map/ppermute | solution.py:321
  19.0 3.2 %collective-permute-start.3 = (f32[192,256]{1,0:T(8,128)S(1)}, f32[192,256]{1,0:T(8,128)S(1)}, u32[]{:S(2)}, u32[]{:S(2)}) collective-permute-start(f32[192,256]{1,0:T(8,128)S(1)} %slice_add_fusion.1), channel_id=1, source_target_pairs={{0,8},{2,10},{4,12},{6,14},{8,0},{10,2},{12,4},{14,6},{16,24},{18,... | collective-permute-start | bytes 589832 | tf_op jit(solution)/shard_map/ppermute | solution.py:321
  22.2 4.5 %collective-permute-done.3.second = f32[192,256]{1,0:T(8,128)S(1)} collective-permute-done((f32[192,256]{1,0:T(8,128)S(1)}, f32[192,256]{1,0:T(8,128)S(1)}, u32[]{:S(2)}, u32[]{:S(2)}) %collective-permute-start.3) | collective-permute-done | bytes 196640 | tf_op jit(solution)/shard_map/ppermute | solution.py:321
  26.7 3.4 %collective-permute-start.4 = (f32[144,256]{1,0:T(8,128)S(1)}, f32[144,256]{1,0:T(8,128)S(1)}, u32[]{:S(2)}, u32[]{:S(2)}) collective-permute-start(f32[144,256]{1,0:T(8,128)S(1)} %slice_add_fusion.2), channel_id=1, source_target_pairs={{0,16},{2,18},{4,20},{6,22},{8,24},{10,26},{12,28},{14,30},{16,0},... | collective-permute-start | bytes 442376 | tf_op jit(solution)/shard_map/ppermute | solution.py:321
  30.0 1.5 %slice.42.right = bf16[2,96,4096]{2,1,0:T(8,128)(2,1)S(1)} slice(bf16[8,96,4096]{2,1,0:T(8,128)(2,1)} %right.1), slice={[6:8], [0:96], [0:4096]} | slice | bytes 3145728 | tf_op jit(solution)/shard_map/slice | solution.py:344
  31.5 0.0 copy-done
  31.6 0.0 copy-start.2
  31.6 0.6 shard_map.67
  32.2 0.0 collective-permute-done.other
  32.2 0.0 slice-start
  32.2 1.2 %shard_map.65.rows = f32[8192,128]{1,0:T(8,128)S(1)} custom-call(f32[32,4096]{1,0:T(8,128)S(1)} %broadcast_divide_fusion.own, f32[32,4096]{1,0:T(8,128)S(1)} %collective-permute-done.other), custom_call_target="tpu_custom_call" | custom-call | flops 262144 | bytes 5242880 | tf_op jit(solution)/shard_map/pallas_call | solution.py:176
  33.4 0.0 copy-done.2
  33.4 0.0 slice-start.1
  33.4 3.8 %shard_map.66 = (bf16[2048,256]{1,0:T(8,128)(2,1)S(1)}, bf16[2048,256]{1,0:T(8,128)(2,1)S(1)}) custom-call(s32[32,128]{1,0:T(8,128)S(1)} %copy-done.2, f32[8192,128]{1,0:T(8,128)S(1)} %shard_map.65.rows), custom_call_target="tpu_custom_call" | custom-call | flops 8388608 | bytes 4194304 | tf_op jit(solution)/shard_map/pallas_call | solution.py:214
  37.2 3.8 %shard_map.70 = (bf16[2048,256]{1,0:T(8,128)(2,1)S(1)}, bf16[2048,256]{1,0:T(8,128)(2,1)S(1)}) custom-call(s32[32,128]{1,0:T(8,128)S(1)} %copy-done.2, f32[8192,128]{1,0:T(8,128)S(1)} %shard_map.65.rows), custom_call_target="tpu_custom_call" | custom-call | flops 8388608 | bytes 4194304 | tf_op jit(solution)/shard_map/pallas_call | solution.py:214
  41.0 0.0 slice-done
  41.0 0.0 slice-done.1
  41.0 1.5 %shard_map.68.near0 = f32[1024,256]{1,0:T(8,128)S(1)} custom-call(bf16[2048,256]{1,0:T(8,128)(2,1)S(1)} %get-tuple-element.16.left, bf16[2048,256]{1,0:T(8,128)(2,1)S(1)} %get-tuple-element.17.right, bf16[4096,256]{1,0:T(8,128)(2,1)S(1)} %copy-done, bf16[8,96,4096]{2,1,0:T(8,128)(2,1)S(1)} %bitcast.6, bf16[2,96,256]{2,1,0:T(8,128)(2,1)S(1)} %get-tuple-element.19.coef7, ...), custom_call_target="tpu_custom_call" | custom-call | flops 1073741824 | bytes 3145728 | tf_op jit(solution)/shard_map/pallas_call | solution.py:246
  42.5 0.0 collective-permute-done.4.third
  42.5 2.0 %collective-permute-start.5 = (f32[96,256]{1,0:T(8,128)S(1)}, f32[96,256]{1,0:T(8,128)S(1)}, u32[]{:S(2)}, u32[]{:S(2)}) collective-permute-start(f32[96,256]{1,0:T(8,128)S(1)} %slice_add_fusion.3), channel_id=1, source_target_pairs={{0,32},{2,34},{4,36},{6,38},{8,40},{10,42},{12,44},{14,46},{16,48}... | collective-permute-start | bytes 294920 | tf_op jit(solution)/shard_map/ppermute | solution.py:321
  44.5 1.5 %shard_map.69.near1 = f32[1024,256]{1,0:T(8,128)S(1)} custom-call(bf16[2048,256]{1,0:T(8,128)(2,1)S(1)} %get-tuple-element.16.left, bf16[2048,256]{1,0:T(8,128)(2,1)S(1)} %get-tuple-element.17.right, bf16[4096,256]{1,0:T(8,128)(2,1)S(1)} %copy-done, bf16[8,96,4096]{2,1,0:T(8,128)(2,1)S(1)} %bitcast.6, bf16[2,96,256]{2,1,0:T(8,128)(2,1)S(1)} %get-tuple-element.19.coef7, ...), custom_call_target="tpu_custom_call" | custom-call | flops 1073741824 | bytes 3145728 | tf_op jit(solution)/shard_map/pallas_call | solution.py:246
  46.0 1.2 %collective-permute-done.5.fourth = f32[96,256]{1,0:T(8,128)S(1)} collective-permute-done((f32[96,256]{1,0:T(8,128)S(1)}, f32[96,256]{1,0:T(8,128)S(1)}, u32[]{:S(2)}, u32[]{:S(2)}) %collective-permute-start.5) | collective-permute-done | bytes 98336 | tf_op jit(solution)/shard_map/ppermute | solution.py:321
  47.2 4.1 %collective-permute-start.6 = (f32[48,256]{1,0:T(8,128)S(1)}, f32[48,256]{1,0:T(8,128)S(1)}, u32[]{:S(2)}, u32[]{:S(2)}) collective-permute-start(f32[48,256]{1,0:T(8,128)S(1)} %get-tuple-element.26), channel_id=1, source_target_pairs={{0,64},{2,66},{4,68},{6,70},{8,72},{10,74},{12,76},{14,78},{16,80}... | collective-permute-start | bytes 147464 | tf_op jit(solution)/shard_map/ppermute | solution.py:321
  51.3 0.3 collective-permute-start.7
  51.6 1.5 %shard_map.71.near2 = f32[1024,256]{1,0:T(8,128)S(1)} custom-call(bf16[2048,256]{1,0:T(8,128)(2,1)S(1)} %get-tuple-element.21.left, bf16[2048,256]{1,0:T(8,128)(2,1)S(1)} %get-tuple-element.22.right, bf16[4096,256]{1,0:T(8,128)(2,1)S(1)} %copy-done, bf16[8,96,4096]{2,1,0:T(8,128)(2,1)S(1)} %bitcast.6, bf16[2,96,256]{2,1,0:T(8,128)(2,1)S(1)} %get-tuple-element.19.coef7, ...), custom_call_target="tpu_custom_call" | custom-call | flops 1073741824 | bytes 3145728 | tf_op jit(solution)/shard_map/pallas_call | solution.py:246
  53.1 0.0 copy-start.1
  53.1 0.3 collective-permute-done.6.fifth
  53.4 0.3 collective-permute-start.8
  53.7 1.5 %shard_map.72.near3 = f32[1024,256]{1,0:T(8,128)S(1)} custom-call(bf16[2048,256]{1,0:T(8,128)(2,1)S(1)} %get-tuple-element.21.left, bf16[2048,256]{1,0:T(8,128)(2,1)S(1)} %get-tuple-element.22.right, bf16[4096,256]{1,0:T(8,128)(2,1)S(1)} %copy-done, bf16[8,96,4096]{2,1,0:T(8,128)(2,1)S(1)} %bitcast.6, bf16[2,96,256]{2,1,0:T(8,128)(2,1)S(1)} %get-tuple-element.19.coef7, ...), custom_call_target="tpu_custom_call" | custom-call | flops 1073741824 | bytes 3145728 | tf_op jit(solution)/shard_map/pallas_call | solution.py:246
  55.2 0.0 collective-permute-done.8.last
  55.2 0.0 collective-permute-done.7.others
  55.2 0.0 copy-done.1
  55.2 9.2 %shard_map.73 = f32[512,2,8,128]{3,2,1,0:T(8,128)} custom-call(s32[32,128]{1,0:T(8,128)S(1)} %bitcast.8, s32[1]{0:T(128)} %bitcast.1.core, f32[1024,256]{1,0:T(8,128)S(1)} %shard_map.68.near0, f32[1024,256]{1,0:T(8,128)S(1)} %shard_map.69.near1, f32[1024,256]{1,0:T(8,128)S(1)} %shard_map.71.near2, f32[1024,256]{1,0:T(8,128)S(1)} %shard_map.72.near3, ...), custom_call_target="tpu_custom_call" | custom-call | flops 1207959552 | bytes 16777216 | tf_op jit(solution)/shard_map/pallas_call | solution.py:304
  (9 shorter events, 0.1 us)
Async XLA Ops:
  0.0 12.5 %copy-start.3 = (f32[32,4096]{1,0:T(8,128)S(1)}, f32[32,4096]{1,0:T(8,128)}, u32[]{:S(2)}) copy-start(f32[32,4096]{1,0:T(8,128)} %param.6) | copy-start | bytes 1572868
  0.0 12.5 %copy-start.4 = (f32[32]{0:T(128)S(1)}, f32[32]{0:T(128)}, u32[]{:S(2)}) copy-start(f32[32]{0:T(128)} %param.7) | copy-start | bytes 388
  7.9 23.6 %copy-start = (bf16[4096,256]{1,0:T(8,128)(2,1)S(1)}, bf16[4096,256]{1,0:T(8,128)(2,1)}, u32[]{:S(2)}) copy-start(bf16[4096,256]{1,0:T(8,128)(2,1)} %get-tuple-element.18.values) | copy-start | bytes 6291460
  7.9 1.9 %collective-permute-start.1 = (f32[336,256]{1,0:T(8,128)}, f32[336,256]{1,0:T(8,128)S(1)}, u32[]{:S(2)}, u32[]{:S(2)}) collective-permute-start(f32[336,256]{1,0:T(8,128)} %get-tuple-element.23), channel_id=1, source_target_pairs={{0,2},{2,0},{4,6},{6,4},{8,10},{10,8},{12,14},{14,12},{16,18},{18,... | collective-permute-start | bytes 1032200 | tf_op jit(solution)/shard_map/ppermute | solution.py:321
  10.8 8.1 %collective-permute-start.2 = (f32[240,256]{1,0:T(8,128)S(1)}, f32[240,256]{1,0:T(8,128)S(1)}, u32[]{:S(2)}, u32[]{:S(2)}) collective-permute-start(f32[240,256]{1,0:T(8,128)S(1)} %slice_add_fusion), channel_id=1, source_target_pairs={{0,4},{2,6},{4,0},{6,2},{8,12},{10,14},{12,8},{14,10},{16,20},{18,... | collective-permute-start | bytes 737288 | tf_op jit(solution)/shard_map/ppermute | solution.py:321
  12.6 19.5 %collective-permute-start = (f32[32,4096]{1,0:T(8,128)S(1)}, f32[32,4096]{1,0:T(8,128)S(1)}, u32[]{:S(2)}, u32[]{:S(2)}) collective-permute-start(f32[32,4096]{1,0:T(8,128)S(1)} %broadcast_divide_fusion.own), channel_id=1, source_target_pairs={{0,1},{1,0},{2,3},{3,2},{4,5},{5,4},{6,7},{7,6},{8,9},{9,8},{10,11... | collective-permute-start | bytes 1572872 | tf_op jit(solution)/shard_map/ppermute | solution.py:328
  19.0 7.7 %collective-permute-start.3 = (f32[192,256]{1,0:T(8,128)S(1)}, f32[192,256]{1,0:T(8,128)S(1)}, u32[]{:S(2)}, u32[]{:S(2)}) collective-permute-start(f32[192,256]{1,0:T(8,128)S(1)} %slice_add_fusion.1), channel_id=1, source_target_pairs={{0,8},{2,10},{4,12},{6,14},{8,0},{10,2},{12,4},{14,6},{16,24},{18,... | collective-permute-start | bytes 589832 | tf_op jit(solution)/shard_map/ppermute | solution.py:321
  26.7 15.8 %collective-permute-start.4 = (f32[144,256]{1,0:T(8,128)S(1)}, f32[144,256]{1,0:T(8,128)S(1)}, u32[]{:S(2)}, u32[]{:S(2)}) collective-permute-start(f32[144,256]{1,0:T(8,128)S(1)} %slice_add_fusion.2), channel_id=1, source_target_pairs={{0,16},{2,18},{4,20},{6,22},{8,24},{10,26},{12,28},{14,30},{16,0},... | collective-permute-start | bytes 442376 | tf_op jit(solution)/shard_map/ppermute | solution.py:321
  31.6 1.8 %copy-start.2 = (s32[32,128]{1,0:T(8,128)S(1)}, s32[32,128]{1,0:T(8,128)}, u32[]{:S(2)}) copy-start(s32[32,128]{1,0:T(8,128)} %get-tuple-element.15.order) | copy-start | bytes 49156
  32.2 8.8 %slice-start = ((s8[6291456]{0:T(1024)(128)(4,1)}), s8[4194304]{0:T(1024)(128)(4,1)S(1)}, s32[]{:S(2)}) async-start(s8[6291456]{0:T(1024)(128)(4,1)} %bitcast.5), calls=%async_computation | async-start | bytes 8388608
  33.4 7.6 %slice-start.1 = ((s8[6291456]{0:T(1024)(128)(4,1)}), s8[2097152]{0:T(1024)(128)(4,1)S(1)}, s32[]{:S(2)}) async-start(s8[6291456]{0:T(1024)(128)(4,1)} %bitcast.5), calls=%async_computation.1 | async-start | bytes 4194304
  42.5 4.7 %collective-permute-start.5 = (f32[96,256]{1,0:T(8,128)S(1)}, f32[96,256]{1,0:T(8,128)S(1)}, u32[]{:S(2)}, u32[]{:S(2)}) collective-permute-start(f32[96,256]{1,0:T(8,128)S(1)} %slice_add_fusion.3), channel_id=1, source_target_pairs={{0,32},{2,34},{4,36},{6,38},{8,40},{10,42},{12,44},{14,46},{16,48}... | collective-permute-start | bytes 294920 | tf_op jit(solution)/shard_map/ppermute | solution.py:321
  47.2 6.2 %collective-permute-start.6 = (f32[48,256]{1,0:T(8,128)S(1)}, f32[48,256]{1,0:T(8,128)S(1)}, u32[]{:S(2)}, u32[]{:S(2)}) collective-permute-start(f32[48,256]{1,0:T(8,128)S(1)} %get-tuple-element.26), channel_id=1, source_target_pairs={{0,64},{2,66},{4,68},{6,70},{8,72},{10,74},{12,76},{14,78},{16,80}... | collective-permute-start | bytes 147464 | tf_op jit(solution)/shard_map/ppermute | solution.py:321
  51.3 3.8 %collective-permute-start.7 = (f32[192,256]{1,0:T(8,128)S(1)}, f32[192,256]{1,0:T(8,128)S(1)}, u32[]{:S(2)}, u32[]{:S(2)}) collective-permute-start(f32[192,256]{1,0:T(8,128)S(1)} %pad_maximum_fusion), channel_id=1, source_target_pairs={{0,2},{2,0},{4,6},{6,4},{8,10},{10,8},{12,14},{14,12},{16,18},{18,... | collective-permute-start | bytes 589832 | tf_op jit(solution)/shard_map/ppermute | solution.py:321
  53.1 2.1 %copy-start.1 = (s32[1,4096]{1,0:T(1,128)S(1)}, s32[1,4096]{1,0:T(1,128)}, u32[]{:S(2)}) copy-start(s32[1,4096]{1,0:T(1,128)} %param.8) | copy-start | bytes 49156
  53.4 1.8 %collective-permute-start.8 = (f32[48,256]{1,0:T(8,128)S(1)}, f32[48,256]{1,0:T(8,128)S(1)}, u32[]{:S(2)}, u32[]{:S(2)}) collective-permute-start(f32[48,256]{1,0:T(8,128)S(1)} %collective-permute-done.6.fifth), channel_id=1, source_target_pairs={{0,2},{2,0},{4,6},{6,4},{8,10},{10,8},{12,14},{14,12},{16,18},{18,... | collective-permute-start | bytes 147464 | tf_op jit(solution)/shard_map/ppermute | solution.py:321
